TPU v7x, 256 devices: a whole 4x4x8 slice. The times are simulated.
256 devices in a mesh: gx: 8 (over y, core), gy: 8 (over z), gz: 4 (over x).
Axes of the slice: x: 4, y: 4, z: 8, core: 2. Of those that a mesh axis runs over, the one named last changes fastest.
Arguments:
- fields: bfloat16 [384, 16, 32, 512], P(None, 'gx', 'gy', 'gz'), may hold values from -6 to 6
- trace_old: float32 [3, 32, 16, 32, 512], P(None, None, 'gx', 'gy', 'gz'), may hold values from -4 to 4
- face_load: float32 [3, 32, 16, 32, 512], P(None, None, 'gx', 'gy', 'gz'), may hold values from -6 to 6
- face_diag: float32 [3, 16, 32, 512], P(None, 'gx', 'gy', 'gz'), may hold values from 0.5 to 4
- fine_flag: int32 [16, 32, 512], P('gx', 'gy', 'gz'), may hold values from 0 to 1
- coeff: float32 [16, 32, 512], P('gx', 'gy', 'gz'), may hold values from 0.5 to 8
- volume_op: bfloat16 [384, 384], replicated, may hold values from -0.3125 to 0.3125
- lift_op: bfloat16 [384, 192], replicated, may hold values from -0.4375 to 0.4375
- schur_op: float32 [192, 192], replicated, may hold values from -8 to 8.5, as said below
Outputs:
- fields_new: bfloat16 [384, 16, 32, 512], P(None, 'gx', 'gy', 'gz')
- trace_new: float32 [3, 32, 16, 32, 512], P(None, None, 'gx', 'gy', 'gz')
Inputs may be any that keep to these rules, and one draw needn't show every extreme that they name: schur_op is symmetric and positive definite.
All inputs are finite; a program needn't handle non-finite values.
Results may differ from a plain program's by a relative error of at most 0.0013.
Values sent between devices are 32-bit elements; how exact they have to be, the bound alone decides.
A program may use at most 64 MiB of HBM per device.

v0:
```python
import functools

import jax
import jax.numpy as jnp
from jax import lax
from jax.sharding import Mesh
from jax.sharding import PartitionSpec as P

ITERS = 2
GX = ("gx_0", "gx_1")
GX_GY_GZ = ("gx_0", "gx_1", "gy", "gz")


time_step = 0.25
highest = lax.Precision.HIGHEST


def from_behind(block, axis, distance):
    devices = range(lax.axis_size(axis))
    route = [(i - distance, i) for i in devices if i - distance in devices]
    return lax.ppermute(block, axis, route)


def one_axis_at_a_time(value, axes):
    return functools.reduce(lax.psum, axes, value)


def padded(value, sides, width):
    for axis, dim in sides:
        size, length = (lax.axis_size(axis), value.shape[dim])
        up = [(i, (i + 1) % size) for i in range(size - 1)]
        down = [(j, i) for i, j in up]
        last = lax.slice_in_dim(value, length - width, length, axis=dim)
        first = lax.slice_in_dim(value, 0, width, axis=dim)
        before = lax.ppermute(last, axis, up)
        after = lax.ppermute(first, axis, down)
        value = jnp.concatenate([before, value, after], axis=dim)
    return value


def upper_extend(values):
    from_x = from_behind(values[0, :, 0:1], GX, -1)
    from_y = from_behind(values[1, :, :, 0:1], "gy", -1)
    from_z = from_behind(values[2, :, :, :, 0:1], "gz", -1)
    wide = jnp.pad(values, ((0, 0), (0, 0), (1, 1), (1, 1), (1, 1)))
    wide = wide.at[0, :, -1:, 1:-1, 1:-1].set(from_x)
    wide = wide.at[1, :, 1:-1, -1:, 1:-1].set(from_y)
    wide = wide.at[2, :, 1:-1, 1:-1, -1:].set(from_z)
    return wide


def extend(values):
    return upper_extend(values)


def owned_coupled(extended, weight, schur_op):
    span_x = extended.shape[2] - 2
    span_y = extended.shape[3] - 2
    span_z = extended.shape[4] - 2
    face_values = own_faces(extended)
    applied = jnp.dot(schur_op, face_values, precision=highest, preferred_element_type=jnp.float32)
    applied = (applied * weight.reshape(1, span_x * span_y * span_z)).reshape(
        6, extended.shape[1], span_x, span_y, span_z
    )
    below_x = from_behind(applied[1][:, -1:], GX, 1)
    below_y = from_behind(applied[3][:, :, -1:], "gy", 1)
    below_z = from_behind(applied[5][:, :, :, -1:], "gz", 1)
    along_x = applied[0] + jnp.concatenate([below_x, applied[1][:, :-1]], 1)
    along_y = applied[2] + jnp.concatenate([below_y, applied[3][:, :, :-1]], 2)
    along_z = applied[4] + jnp.concatenate([below_z, applied[5][:, :, :, :-1]], 3)
    return jnp.stack([along_x, along_y, along_z], 0)


def own_faces(extended):
    span_x = extended.shape[2] - 2
    span_y = extended.shape[3] - 2
    span_z = extended.shape[4] - 2
    pieces = [
        extended[0, :, 1 : span_x + 1, 1 : span_y + 1, 1 : span_z + 1],
        extended[0, :, 2 : span_x + 2, 1 : span_y + 1, 1 : span_z + 1],
        extended[1, :, 1 : span_x + 1, 1 : span_y + 1, 1 : span_z + 1],
        extended[1, :, 1 : span_x + 1, 2 : span_y + 2, 1 : span_z + 1],
        extended[2, :, 1 : span_x + 1, 1 : span_y + 1, 1 : span_z + 1],
        extended[2, :, 1 : span_x + 1, 1 : span_y + 1, 2 : span_z + 2],
    ]
    face_values = jnp.concatenate(pieces, 0)
    return face_values.reshape(face_values.shape[0], span_x * span_y * span_z)


def both_products(residual, applied):
    return (
        one_axis_at_a_time(jnp.sum(residual * residual), GX_GY_GZ),
        one_axis_at_a_time(jnp.sum(residual * applied), GX_GY_GZ),
    )


def body(fields, trace_old, face_load, face_diag, fine_flag, coeff, volume_op, lift_op, schur_op):
    fine_mask = fine_flag.astype(jnp.float32)
    weight = fine_mask * coeff
    wide_old, weight_wide = (
        padded(trace_old, ((GX, 2), ("gy", 3), ("gz", 4)), 1),
        padded(weight[None, None], ((GX, 2), ("gy", 3), ("gz", 4)), 1),
    )

    def operate(extended, traces):
        return face_diag[:, None] * traces + owned_coupled(extended, weight, schur_op)

    solution = trace_old
    wide_solution = wide_old
    residual = face_load - operate(wide_old, trace_old)
    wide_residual = extend(residual)
    applied = operate(wide_residual, residual)
    norm_now, product = both_products(residual, applied)
    step_length = norm_now / product
    direction, along, wide_direction = (residual, applied, wide_residual)
    for iteration in range(ITERS):
        solution = solution + step_length * direction
        wide_solution = wide_solution + step_length * wide_direction
        if iteration + 1 < ITERS:
            residual = residual - step_length * along
            wide_residual = extend(residual)
            applied = operate(wide_residual, residual)
            norm_next, product = both_products(residual, applied)
            beta_ratio = norm_next / norm_now
            step_length = norm_next / (product - beta_ratio * norm_next / step_length)
            direction = residual + beta_ratio * direction
            along = applied + beta_ratio * along
            wide_direction = wide_residual + beta_ratio * wide_direction
            norm_now = norm_next
    cells = fine_mask.size
    fine_row = fine_mask.reshape(1, cells)
    traced = fine_row * own_faces(wide_solution) + (1.0 - fine_row) * own_faces(wide_old)
    nodal = fields.reshape(fields.shape[0], cells)
    volume = jnp.dot(volume_op, nodal, preferred_element_type=jnp.float32)
    lifted = jnp.dot(lift_op, traced.astype(jnp.bfloat16), preferred_element_type=jnp.float32)
    result = nodal.astype(jnp.float32) + time_step * ((1.0 - fine_row) * volume + lifted)
    return (result.astype(jnp.bfloat16).reshape(fields.shape), solution)


def solution(mesh):
    torus = Mesh(
        mesh.devices.reshape(4, 2, mesh.shape["gy"], mesh.shape["gz"]), ("gx_0", "gx_1", "gy", "gz")
    )
    return jax.shard_map(
        body,
        mesh=torus,
        in_specs=(
            P(None, GX, "gy", "gz"),
            P(None, None, GX, "gy", "gz"),
            P(None, None, GX, "gy", "gz"),
            P(None, GX, "gy", "gz"),
            P(GX, "gy", "gz"),
            P(GX, "gy", "gz"),
            P(),
            P(),
            P(),
        ),
        out_specs=(P(None, GX, "gy", "gz"), P(None, None, GX, "gy", "gz")),
        check_vma=False,
    )
```

profile of v0, /device:TPU:8, one launch (start us, length us, event | category | flops | bytes accessed | tf_op | source)
XLA Modules:
  0.0 330.2 jit_solution(15551347898626678459)
XLA Ops:
  1.8 1.9 collective-permute-start.1
  3.8 2.4 collective-permute-start
  6.9 2.3 reshape.706
  9.3 2.1 collective-permute-done
  11.5 3.3 collective-permute-start.2
  16.5 2.2 collective-permute-done.2
  18.8 4.3 %collective-permute-done.3 = f32[3,32,4,1,128]{4,1,3,2,0:T(8,128)S(1)} collective-permute-done((f32[3,32,4,1,128]{4,1,3,2,0:T(8,128)S(1)}, f32[3,32,4,1,128]{4,1,3,2,0:T(8,128)S(1)}, u32[]{:S(2)}, u32[]{:S(2)}) %collective-permute-start.3) | collective-permute-done | bytes 196640 | tf_op jit(solution)/shard_map/ppermute | solution.py:36
  27.2 3.9 %collective-permute-done.5 = f32[3,32,4,6,1]{1,2,4,3,0:T(4,128)} collective-permute-done((f32[3,32,4,6,1]{1,2,4,3,0:T(4,128)S(1)}, f32[3,32,4,6,1]{1,2,4,3,0:T(4,128)}, u32[]{:S(2)}, u32[]{:S(2)}) %collective-permute-start.5) | collective-permute-done | bytes 9248 | tf_op jit(solution)/shard_map/ppermute | solution.py:36
  34.9 2.0 fusion.7
  37.4 3.4 %collective-permute-start.8 = (f32[32,2,4,1]{0,2,3,1:T(4,128)S(1)}, f32[32,2,4,1]{0,2,3,1:T(4,128)S(1)}, u32[]{:S(2)}, u32[]{:S(2)}) collective-permute-start(f32[32,2,4,1]{0,2,3,1:T(4,128)S(1)} %copy.209), channel_id=1, source_target_pairs={{0,1},{1,2},{2,3},{4,5},{5,6},{6,7},{8,9},{9,10},{10,11},{12,13},{... | collective-permute-start | bytes 3080 | tf_op jit(solution)/shard_map/ppermute | solution.py:21
  40.8 1.9 collective-permute-start.6
  42.9 4.0 %collective-permute-start.7 = (f32[32,2,1,128]{3,0,1,2:T(8,128)S(1)}, f32[32,2,1,128]{3,0,1,2:T(8,128)S(1)}, u32[]{:S(2)}, u32[]{:S(2)}) collective-permute-start(f32[32,2,1,128]{3,0,1,2:T(8,128)S(1)} %copy.207), channel_id=1, source_target_pairs={{0,4},{4,8},{8,12},{12,16},{16,20},{20,24},{24,28},{1,5},{5,9},{9,... | collective-permute-start | bytes 98312 | tf_op jit(solution)/shard_map/ppermute | solution.py:21
  49.9 2.8 collective-permute-start.9
  55.4 1.7 fusion.26
  58.3 5.2 %collective-permute-start.4 = (f32[3,32,4,6,1]{1,2,4,3,0:T(4,128)}, f32[3,32,4,6,1]{1,2,4,3,0:T(4,128)}, u32[]{:S(2)}, u32[]{:S(2)}) collective-permute-start(f32[3,32,4,6,1]{1,2,4,3,0:T(4,128)} %copy.134), channel_id=1, source_target_pairs={{0,1},{1,2},{2,3},{4,5},{5,6},{6,7},{8,9},{9,10},{10,11},{12,13},{... | collective-permute-start | bytes 27656 | tf_op jit(solution)/shard_map/ppermute | solution.py:35
  63.4 1.9 pad.31
  66.1 2.1 scatter.20
  68.2 1.8 copy.156
  70.7 1.6 scatter.24
  77.6 1.6 copy.160
  80.8 1.6 copy.161
  84.0 1.6 copy.162
  87.3 1.6 copy.163
  88.9 1.6 concatenate.250
  90.5 1.6 copy.164
  101.6 2.0 fusion.6
  104.2 2.8 collective-permute-start.14
  107.0 1.9 collective-permute-start.12
  109.1 5.7 %collective-permute-start.13 = (f32[32,2,1,128]{3,0,1,2:T(8,128)S(1)}, f32[32,2,1,128]{3,0,1,2:T(8,128)S(1)}, u32[]{:S(2)}, u32[]{:S(2)}) collective-permute-start(f32[32,2,1,128]{3,0,1,2:T(8,128)S(1)} %copy.213), channel_id=1, source_target_pairs={{0,4},{4,8},{8,12},{12,16},{16,20},{20,24},{24,28},{1,5},{5,9},{9,... | collective-permute-start | bytes 98312 | tf_op jit(solution)/shard_map/ppermute | solution.py:21
  117.3 9.4 %all-reduce.7 = (f32[]{:T(128)}, f32[]{:T(128)}) all-reduce(f32[]{:T(128)} %get-tuple-element.81, f32[]{:T(128)} %get-tuple-element.80), channel_id=1, replica_groups=mesh['gx_0'=4,'gx_1'=2,'gy'=8,'gz'=4] {'gx_0'}, use_global_device_ids=true, to_apply=%region_1.2 | all-reduce | flops 2 | bytes 16 | tf_op jit(solution)/shard_map/psum | solution.py:25
  126.6 3.1 all-reduce.9
  129.7 20.3 %all-reduce.3 = (f32[]{:T(128)}, f32[]{:T(128)}) all-reduce(f32[]{:T(128)} %get-tuple-element.96, f32[]{:T(128)} %get-tuple-element.97), channel_id=1, replica_groups=mesh['gx_0'=4,'gx_1'=2,'gy'=8,'gz'=4] {'gy'}, use_global_device_ids=true, to_apply=%region_3.4 | all-reduce | flops 2 | bytes 16 | tf_op jit(solution)/shard_map/psum | solution.py:25
  150.0 8.4 %all-reduce.5 = (f32[]{:T(128)}, f32[]{:T(128)}) all-reduce(f32[]{:T(128)} %get-tuple-element.84, f32[]{:T(128)} %get-tuple-element.85), channel_id=1, replica_groups=mesh['gx_0'=4,'gx_1'=2,'gy'=8,'gz'=4] {'gz'}, use_global_device_ids=true, to_apply=%region_4.5 | all-reduce | flops 2 | bytes 16 | tf_op jit(solution)/shard_map/psum | solution.py:25
  160.6 2.1 collective-permute-start.15
  165.5 2.3 copy.136
  173.3 1.6 scatter.29
  179.9 1.6 copy.179
  183.2 1.6 copy.180
  186.4 1.6 copy.181
  189.7 1.6 copy.182
  193.0 1.6 copy.183
  204.0 2.0 fusion.5
  206.9 1.6 squeeze.130
  211.7 1.7 slice.634
  214.4 4.1 %collective-permute-start.20 = (f32[32,2,4,1]{0,2,3,1:T(4,128)S(1)}, f32[32,2,4,1]{0,2,3,1:T(4,128)S(1)}, u32[]{:S(2)}, u32[]{:S(2)}) collective-permute-start(f32[32,2,4,1]{0,2,3,1:T(4,128)S(1)} %copy.221), channel_id=1, source_target_pairs={{0,1},{1,2},{2,3},{4,5},{5,6},{6,7},{8,9},{9,10},{10,11},{12,13},{... | collective-permute-start | bytes 3080 | tf_op jit(solution)/shard_map/ppermute | solution.py:21
  219.1 1.9 collective-permute-start.18
  223.5 1.6 squeeze.132
  226.7 5.1 %collective-permute-start.19 = (f32[32,2,1,128]{3,0,1,2:T(8,128)}, f32[32,2,1,128]{3,0,1,2:T(8,128)}, u32[]{:S(2)}, u32[]{:S(2)}) collective-permute-start(f32[32,2,1,128]{3,0,1,2:T(8,128)} %copy.219), channel_id=1, source_target_pairs={{0,4},{4,8},{8,12},{12,16},{16,20},{20,24},{24,28},{1,5},{5,9},{9,... | collective-permute-start | bytes 98312 | tf_op jit(solution)/shard_map/ppermute | solution.py:21
  233.4 1.6 squeeze.131
  242.2 1.8 fusion.10
  243.9 11.3 %all-reduce.6 = (f32[]{:T(128)}, f32[]{:T(128)}) all-reduce(f32[]{:T(128)} %get-tuple-element.79, f32[]{:T(128)} %get-tuple-element.78), channel_id=1, replica_groups=mesh['gx_0'=4,'gx_1'=2,'gy'=8,'gz'=4] {'gx_0'}, use_global_device_ids=true, to_apply=%region_11.12 | all-reduce | flops 2 | bytes 16 | tf_op jit(solution)/shard_map/psum | solution.py:25
  255.2 3.1 all-reduce.8
  258.3 17.1 %all-reduce.2 = (f32[]{:T(128)}, f32[]{:T(128)}) all-reduce(f32[]{:T(128)} %get-tuple-element.94, f32[]{:T(128)} %get-tuple-element.95), channel_id=1, replica_groups=mesh['gx_0'=4,'gx_1'=2,'gy'=8,'gz'=4] {'gy'}, use_global_device_ids=true, to_apply=%region_13.14 | all-reduce | flops 2 | bytes 16 | tf_op jit(solution)/shard_map/psum | solution.py:25
  275.4 10.1 %all-reduce.4 = (f32[]{:T(128)}, f32[]{:T(128)}) all-reduce(f32[]{:T(128)} %get-tuple-element.82, f32[]{:T(128)} %get-tuple-element.83), channel_id=1, replica_groups=mesh['gx_0'=4,'gx_1'=2,'gy'=8,'gz'=4] {'gz'}, use_global_device_ids=true, to_apply=%region_14.15 | all-reduce | flops 2 | bytes 16 | tf_op jit(solution)/shard_map/psum | solution.py:25
  292.3 3.2 fusion
  297.4 1.9 concatenate.278
  300.8 1.7 copy.196
  304.1 1.7 copy.197
  307.4 1.7 copy.198
  310.6 1.7 copy.199
  312.3 1.6 concatenate.282
  313.9 1.7 copy.200
  325.0 2.6 fusion.4
  327.6 2.6 reshape.714
  (212 shorter events, 111.0 us)
Async XLA Ops:
  0.6 54.8 %copy-start = (bf16[384,384]{1,0:T(8,128)(2,1)S(1)}, bf16[384,384]{1,0:T(8,128)(2,1)}, u32[]{:S(2)}) copy-start(bf16[384,384]{1,0:T(8,128)(2,1)} %param.27) | copy-start | bytes 884740
  0.6 10.7 %copy-start.1 = (f32[3,32,2,4,128]{4,3,2,1,0:T(4,128)S(1)}, f32[3,32,2,4,128]{4,3,2,1,0:T(4,128)}, u32[]{:S(2)}) copy-start(f32[3,32,2,4,128]{4,3,2,1,0:T(4,128)} %param.22) | copy-start | bytes 1179652
  0.7 8.6 %copy-start.20 = (f32[2,4,128]{2,1,0:T(4,128)S(1)}, f32[2,4,128]{2,1,0:T(4,128)}, u32[]{:S(2)}) copy-start(f32[2,4,128]{2,1,0:T(4,128)} %param.26) | copy-start | bytes 12292
  0.7 8.6 %copy-start.19 = (s32[2,4,128]{2,1,0:T(4,128)S(1)}, s32[2,4,128]{2,1,0:T(4,128)}, u32[]{:S(2)}) copy-start(s32[2,4,128]{2,1,0:T(4,128)} %param.25) | copy-start | bytes 12292
  1.8 9.6 %collective-permute-start.1 = (f32[3,32,1,4,128]{4,1,3,2,0:T(8,128)S(1)}, f32[3,32,1,4,128]{4,1,3,2,0:T(8,128)S(1)}, u32[]{:S(2)}, u32[]{:S(2)}) collective-permute-start(f32[3,32,1,4,128]{4,1,3,2,0:T(8,128)S(1)} %copy.250), channel_id=1, source_target_pairs={{32,0},{64,32},{96,64},{128,96},{160,128},{192,160},{224,192},{33,... | collective-permute-start | bytes 589832 | tf_op jit(solution)/shard_map/ppermute | solution.py:36
  3.8 7.5 %collective-permute-start = (f32[3,32,1,4,128]{4,1,3,2,0:T(8,128)S(1)}, f32[3,32,1,4,128]{4,1,3,2,0:T(8,128)S(1)}, u32[]{:S(2)}, u32[]{:S(2)}) collective-permute-start(f32[3,32,1,4,128]{4,1,3,2,0:T(8,128)S(1)} %copy.251), channel_id=1, source_target_pairs={{0,32},{32,64},{64,96},{96,128},{128,160},{160,192},{192,224},{1,3... | collective-permute-start | bytes 589832 | tf_op jit(solution)/shard_map/ppermute | solution.py:35
  11.4 20.9 %copy-start.4 = (f32[3,32,4,4,128]{4,1,3,2,0:T(8,128)}, f32[3,32,4,4,128]{4,1,3,2,0:T(8,128)S(1)}, u32[]{:S(2)}) copy-start(f32[3,32,4,4,128]{4,1,3,2,0:T(8,128)S(1)} %constant_dynamic-update-slice_fusion) | copy-start | bytes 2359300
  11.5 7.3 %collective-permute-start.2 = (f32[3,32,4,1,128]{4,1,3,2,0:T(8,128)S(1)}, f32[3,32,4,1,128]{4,1,3,2,0:T(8,128)S(1)}, u32[]{:S(2)}, u32[]{:S(2)}) collective-permute-start(f32[3,32,4,1,128]{4,1,3,2,0:T(8,128)S(1)} %get-tuple-element.138), channel_id=1, source_target_pairs={{0,4},{4,8},{8,12},{12,16},{16,20},{20,24},{24,28},{1,5},{5,9},{9,... | collective-permute-start | bytes 589832 | tf_op jit(solution)/shard_map/ppermute | solution.py:35
  14.8 8.3 %collective-permute-start.3 = (f32[3,32,4,1,128]{4,1,3,2,0:T(8,128)S(1)}, f32[3,32,4,1,128]{4,1,3,2,0:T(8,128)S(1)}, u32[]{:S(2)}, u32[]{:S(2)}) collective-permute-start(f32[3,32,4,1,128]{4,1,3,2,0:T(8,128)S(1)} %get-tuple-element.139), channel_id=1, source_target_pairs={{4,0},{8,4},{12,8},{16,12},{20,16},{24,20},{28,24},{5,1},{9,5},{13... | collective-permute-start | bytes 589832 | tf_op jit(solution)/shard_map/ppermute | solution.py:36
  16.5 2.3 copy-start.10
  18.8 13.6 %copy-start.17 = (f32[3,32,4,1,128]{4,1,3,2,0:T(8,128)}, f32[3,32,4,1,128]{4,1,3,2,0:T(8,128)S(1)}, u32[]{:S(2)}) copy-start(f32[3,32,4,1,128]{4,1,3,2,0:T(8,128)S(1)} %collective-permute-done.2) | copy-start | bytes 589828
  23.1 9.3 %copy-start.18 = (f32[3,32,4,1,128]{4,1,3,2,0:T(8,128)}, f32[3,32,4,1,128]{4,1,3,2,0:T(8,128)S(1)}, u32[]{:S(2)}) copy-start(f32[3,32,4,1,128]{4,1,3,2,0:T(8,128)S(1)} %collective-permute-done.3) | copy-start | bytes 589828
  25.1 6.0 %collective-permute-start.5 = (f32[3,32,4,6,1]{1,2,4,3,0:T(4,128)S(1)}, f32[3,32,4,6,1]{1,2,4,3,0:T(4,128)}, u32[]{:S(2)}, u32[]{:S(2)}) collective-permute-start(f32[3,32,4,6,1]{1,2,4,3,0:T(4,128)S(1)} %copy.135), channel_id=1, source_target_pairs={{1,0},{2,1},{3,2},{5,4},{6,5},{7,6},{9,8},{10,9},{11,10},{13,12},{... | collective-permute-start | bytes 27656 | tf_op jit(solution)/shard_map/ppermute | solution.py:36
  32.4 4.5 %copy-start.5 = (f32[3,32,4,6,1]{4,1,3,2,0:T(8,128)}, f32[3,32,4,6,1]{4,1,3,2,0:T(8,128)S(1)}, u32[]{:S(2)}) copy-start(f32[3,32,4,6,1]{4,1,3,2,0:T(8,128)S(1)} %copy.137) | copy-start | bytes 27652
  32.4 2.5 copy-start.16
  37.4 9.7 %collective-permute-start.8 = (f32[32,2,4,1]{0,2,3,1:T(4,128)S(1)}, f32[32,2,4,1]{0,2,3,1:T(4,128)S(1)}, u32[]{:S(2)}, u32[]{:S(2)}) collective-permute-start(f32[32,2,4,1]{0,2,3,1:T(4,128)S(1)} %copy.209), channel_id=1, source_target_pairs={{0,1},{1,2},{2,3},{4,5},{5,6},{6,7},{8,9},{9,10},{10,11},{12,13},{... | collective-permute-start | bytes 3080 | tf_op jit(solution)/shard_map/ppermute | solution.py:21
  40.8 7.7 %collective-permute-start.6 = (f32[32,1,4,128]{3,0,2,1:T(8,128)S(1)}, f32[32,1,4,128]{3,0,2,1:T(8,128)S(1)}, u32[]{:S(2)}, u32[]{:S(2)}) collective-permute-start(f32[32,1,4,128]{3,0,2,1:T(8,128)S(1)} %copy.205), channel_id=1, source_target_pairs={{0,32},{32,64},{64,96},{96,128},{128,160},{160,192},{192,224},{1,3... | collective-permute-start | bytes 196616 | tf_op jit(solution)/shard_map/ppermute | solution.py:21
  42.9 12.5 %copy-start.6 = (bf16[384,1024]{1,0:T(8,128)(2,1)S(1)}, bf16[384,1024]{1,0:T(8,128)(2,1)}, u32[]{:S(2)}) copy-start(bf16[384,1024]{1,0:T(8,128)(2,1)} %reshape.706) | copy-start | bytes 2359300
  42.9 5.5 %collective-permute-start.7 = (f32[32,2,1,128]{3,0,1,2:T(8,128)S(1)}, f32[32,2,1,128]{3,0,1,2:T(8,128)S(1)}, u32[]{:S(2)}, u32[]{:S(2)}) collective-permute-start(f32[32,2,1,128]{3,0,1,2:T(8,128)S(1)} %copy.207), channel_id=1, source_target_pairs={{0,4},{4,8},{8,12},{12,16},{16,20},{20,24},{24,28},{1,5},{5,9},{9,... | collective-permute-start | bytes 98312 | tf_op jit(solution)/shard_map/ppermute | solution.py:21
  48.6 8.6 %copy-start.9 = (f32[3,32,4,6,1]{4,1,3,2,0:T(8,128)S(1)}, f32[3,32,4,6,1]{4,1,3,2,0:T(8,128)}, u32[]{:S(2)}) copy-start(f32[3,32,4,6,1]{4,1,3,2,0:T(8,128)} %get-tuple-element.116) | copy-start | bytes 27652
  49.9 16.2 %collective-permute-start.9 = (f32[32,1,4,128]{3,0,2,1:T(8,128)S(1)}, f32[32,1,4,128]{3,0,2,1:T(8,128)S(1)}, u32[]{:S(2)}, u32[]{:S(2)}) collective-permute-start(f32[32,1,4,128]{3,0,2,1:T(8,128)S(1)} %slice_bitcast_fusion.1), channel_id=1, source_target_pairs={{32,0},{64,32},{96,64},{128,96},{160,128},{192,160},{224,192},{33,... | collective-permute-start | bytes 196616 | tf_op jit(solution)/shard_map/ppermute | solution.py:21
  52.7 17.4 %collective-permute-start.10 = (f32[32,2,1,128]{3,0,1,2:T(8,128)S(1)}, f32[32,2,1,128]{3,0,1,2:T(8,128)S(1)}, u32[]{:S(2)}, u32[]{:S(2)}) collective-permute-start(f32[32,2,1,128]{3,0,1,2:T(8,128)S(1)} %slice_bitcast_fusion.3), channel_id=1, source_target_pairs={{4,0},{8,4},{12,8},{16,12},{20,16},{24,20},{28,24},{5,1},{9,5},{13... | collective-permute-start | bytes 98312 | tf_op jit(solution)/shard_map/ppermute | solution.py:21
  54.1 11.2 %collective-permute-start.11 = (f32[32,2,4,1]{0,2,3,1:T(4,128)S(1)}, f32[32,2,4,1]{0,2,3,1:T(4,128)S(1)}, u32[]{:S(2)}, u32[]{:S(2)}) collective-permute-start(f32[32,2,4,1]{0,2,3,1:T(4,128)S(1)} %bitcast.121), channel_id=1, source_target_pairs={{1,0},{2,1},{3,2},{5,4},{6,5},{7,6},{9,8},{10,9},{11,10},{13,12},{... | collective-permute-start | bytes 3080 | tf_op jit(solution)/shard_map/ppermute | solution.py:21
  58.3 107.2 %collective-permute-start.4 = (f32[3,32,4,6,1]{1,2,4,3,0:T(4,128)}, f32[3,32,4,6,1]{1,2,4,3,0:T(4,128)}, u32[]{:S(2)}, u32[]{:S(2)}) collective-permute-start(f32[3,32,4,6,1]{1,2,4,3,0:T(4,128)} %copy.134), channel_id=1, source_target_pairs={{0,1},{1,2},{2,3},{4,5},{5,6},{6,7},{8,9},{9,10},{10,11},{12,13},{... | collective-permute-start | bytes 27656 | tf_op jit(solution)/shard_map/ppermute | solution.py:35
  72.3 19.9 %copy-start.2 = (f32[3,32,4,6,130]{4,1,3,2,0:T(8,128)}, f32[3,32,4,6,130]{4,1,3,2,0:T(8,128)S(1)}, u32[]{:S(2)}) copy-start(f32[3,32,4,6,130]{4,1,3,2,0:T(8,128)S(1)} %scatter.24) | copy-start | bytes 3594244
  104.2 10.8 %collective-permute-start.14 = (f32[32,2,4,1]{0,2,3,1:T(4,128)S(1)}, f32[32,2,4,1]{0,2,3,1:T(4,128)S(1)}, u32[]{:S(2)}, u32[]{:S(2)}) collective-permute-start(f32[32,2,4,1]{0,2,3,1:T(4,128)S(1)} %copy.215), channel_id=1, source_target_pairs={{0,1},{1,2},{2,3},{4,5},{5,6},{6,7},{8,9},{9,10},{10,11},{12,13},{... | collective-permute-start | bytes 3080 | tf_op jit(solution)/shard_map/ppermute | solution.py:21
  107.0 9.4 %collective-permute-start.12 = (f32[32,1,4,128]{3,0,2,1:T(8,128)S(1)}, f32[32,1,4,128]{3,0,2,1:T(8,128)S(1)}, u32[]{:S(2)}, u32[]{:S(2)}) collective-permute-start(f32[32,1,4,128]{3,0,2,1:T(8,128)S(1)} %copy.211), channel_id=1, source_target_pairs={{0,32},{32,64},{64,96},{96,128},{128,160},{160,192},{192,224},{1,3... | collective-permute-start | bytes 196616 | tf_op jit(solution)/shard_map/ppermute | solution.py:21
  109.1 7.2 %collective-permute-start.13 = (f32[32,2,1,128]{3,0,1,2:T(8,128)S(1)}, f32[32,2,1,128]{3,0,1,2:T(8,128)S(1)}, u32[]{:S(2)}, u32[]{:S(2)}) collective-permute-start(f32[32,2,1,128]{3,0,1,2:T(8,128)S(1)} %copy.213), channel_id=1, source_target_pairs={{0,4},{4,8},{8,12},{12,16},{16,20},{20,24},{24,28},{1,5},{5,9},{9,... | collective-permute-start | bytes 98312 | tf_op jit(solution)/shard_map/ppermute | solution.py:21
  115.3 50.2 %copy-start.14 = (f32[1,32,2,4,128]{4,1,2,3,0:T(8,128)}, f32[1,32,2,4,128]{4,1,2,3,0:T(8,128)S(1)}, u32[]{:S(2)}) copy-start(f32[1,32,2,4,128]{4,1,2,3,0:T(8,128)S(1)} %maximum_add_fusion.9) | copy-start | bytes 393220
  116.4 49.0 %copy-start.12 = (f32[1,32,2,4,128]{4,1,2,3,0:T(8,128)}, f32[1,32,2,4,128]{4,1,2,3,0:T(8,128)S(1)}, u32[]{:S(2)}) copy-start(f32[1,32,2,4,128]{4,1,2,3,0:T(8,128)S(1)} %maximum_add_fusion.8) | copy-start | bytes 393220
  116.5 49.0 %copy-start.13 = (f32[1,32,2,4,128]{4,1,2,3,0:T(8,128)}, f32[1,32,2,4,128]{4,1,2,3,0:T(8,128)S(1)}, u32[]{:S(2)}) copy-start(f32[1,32,2,4,128]{4,1,2,3,0:T(8,128)S(1)} %maximum_add_fusion.7) | copy-start | bytes 393220
  159.8 0.8 copy-start.15
  160.6 9.8 %collective-permute-start.15 = (f32[32,1,4,128]{3,0,2,1:T(8,128)S(1)}, f32[32,1,4,128]{3,0,2,1:T(8,128)}, u32[]{:S(2)}, u32[]{:S(2)}) collective-permute-start(f32[32,1,4,128]{3,0,2,1:T(8,128)S(1)} %slice_bitcast_fusion), channel_id=1, source_target_pairs={{32,0},{64,32},{96,64},{128,96},{160,128},{192,160},{224,192},{33,... | collective-permute-start | bytes 196616 | tf_op jit(solution)/shard_map/ppermute | solution.py:21
  162.7 9.3 %collective-permute-start.16 = (f32[32,2,1,128]{3,0,1,2:T(8,128)}, f32[32,2,1,128]{3,0,1,2:T(8,128)}, u32[]{:S(2)}, u32[]{:S(2)}) collective-permute-start(f32[32,2,1,128]{3,0,1,2:T(8,128)} %slice_bitcast_fusion.2), channel_id=1, source_target_pairs={{4,0},{8,4},{12,8},{16,12},{20,16},{24,20},{28,24},{5,1},{9,5},{13... | collective-permute-start | bytes 98312 | tf_op jit(solution)/shard_map/ppermute | solution.py:21
  164.1 5.5 %collective-permute-start.17 = (f32[32,2,4,1]{0,2,3,1:T(4,128)S(1)}, f32[32,2,4,1]{0,2,3,1:T(4,128)S(1)}, u32[]{:S(2)}, u32[]{:S(2)}) collective-permute-start(f32[32,2,4,1]{0,2,3,1:T(4,128)S(1)} %bitcast.123), channel_id=1, source_target_pairs={{1,0},{2,1},{3,2},{5,4},{6,5},{7,6},{9,8},{10,9},{11,10},{13,12},{... | collective-permute-start | bytes 3080 | tf_op jit(solution)/shard_map/ppermute | solution.py:21
  214.4 23.9 %collective-permute-start.20 = (f32[32,2,4,1]{0,2,3,1:T(4,128)S(1)}, f32[32,2,4,1]{0,2,3,1:T(4,128)S(1)}, u32[]{:S(2)}, u32[]{:S(2)}) collective-permute-start(f32[32,2,4,1]{0,2,3,1:T(4,128)S(1)} %copy.221), channel_id=1, source_target_pairs={{0,1},{1,2},{2,3},{4,5},{5,6},{6,7},{8,9},{9,10},{10,11},{12,13},{... | collective-permute-start | bytes 3080 | tf_op jit(solution)/shard_map/ppermute | solution.py:21
  219.1 22.0 %collective-permute-start.18 = (f32[32,1,4,128]{3,0,2,1:T(8,128)}, f32[32,1,4,128]{3,0,2,1:T(8,128)}, u32[]{:S(2)}, u32[]{:S(2)}) collective-permute-start(f32[32,1,4,128]{3,0,2,1:T(8,128)} %copy.217), channel_id=1, source_target_pairs={{0,32},{32,64},{64,96},{96,128},{128,160},{160,192},{192,224},{1,3... | collective-permute-start | bytes 196616 | tf_op jit(solution)/shard_map/ppermute | solution.py:21
  226.7 13.5 %collective-permute-start.19 = (f32[32,2,1,128]{3,0,1,2:T(8,128)}, f32[32,2,1,128]{3,0,1,2:T(8,128)}, u32[]{:S(2)}, u32[]{:S(2)}) collective-permute-start(f32[32,2,1,128]{3,0,1,2:T(8,128)} %copy.219), channel_id=1, source_target_pairs={{0,4},{4,8},{8,12},{12,16},{16,20},{20,24},{24,28},{1,5},{5,9},{9,... | collective-permute-start | bytes 98312 | tf_op jit(solution)/shard_map/ppermute | solution.py:21
  290.0 2.4 copy-start.3
  296.6 28.3 %copy-start.7 = (bf16[384,1024]{1,0:T(8,128)(2,1)S(1)}, bf16[384,1024]{1,0:T(8,128)(2,1)}, u32[]{:S(2)}) copy-start(bf16[384,1024]{1,0:T(8,128)(2,1)} %reshape.706) | copy-start | bytes 2359300
  296.6 28.3 %copy-start.8 = (f32[384,1024]{1,0:T(8,128)S(1)}, f32[384,1024]{1,0:T(8,128)}, u32[]{:S(2)}) copy-start(f32[384,1024]{1,0:T(8,128)} %fusion.26) | copy-start | bytes 4718596
  296.7 28.3 %copy-start.11 = (f32[192,1024]{1,0:T(8,128)S(1)}, f32[192,1024]{1,0:T(8,128)}, u32[]{:S(2)}) copy-start(f32[192,1024]{1,0:T(8,128)} %constant_dynamic-update-slice_fusion.3) | copy-start | bytes 2359300
where the time goes:
time: 333 us; the launch traced here: 330 us
  local copies, waits for them, and re-layouts  146 us (44%)
  blocking collectives  82.8 us (25%)
  starting transfers between devices  56.2 us (17%)
  waiting for transfers between devices  15.2 us (5%)
  other arithmetic  12.2 us (4%)
  matrix products  10.3 us (3%)
  between operations  7.42 us (2%)
    psum x8, blocking collectives, one_axis_at_a_time(): return functools.reduce(lax.psum, axes, value)  82.8 us
    ppermute x15, starting transfers between devices, from_behind(): return lax.ppermute(block, axis, route)  40.9 us
    concatenate x28, local copies, waits for them, and re-layouts, own_faces(): face_values = jnp.concatenate(pieces, 0)  34.9 us
    unnamed x86, local copies, waits for them, and re-layouts  34.2 us
    ppermute x3, starting transfers between devices, padded(): before = lax.ppermute(last, axis, up)  10.8 us
    slice x7, local copies, waits for them, and re-layouts, own_faces(): extended[2, :, 1:span_x + 1, 1:span_y + 1, 2:span_z + 2]  8.52 us
    ppermute x3, waiting for transfers between devices, padded(): after = lax.ppermute(first, axis, down)  8.24 us
  transfers between devices with their start and end apart: 21, of which 7 were waited for; matrix products, arithmetic and copies ran while one was open for 22% of the time, Pallas kernels for 0%

commit v1 on v0

v1 whole, which is shorter than its diff:
```python
import functools

import jax
import jax.numpy as jnp
from jax import lax
from jax.experimental import pallas as pl
from jax.experimental.pallas import tpu as pltpu
from jax.sharding import PartitionSpec as P

MESH = pl.DeviceIdType.MESH
EX, EY, EZ = 2, 4, 128
CELLS = EX * EY
FD = 32
F32, BF16 = jnp.float32, jnp.bfloat16
TIME_STEP = 0.25


def dot(a, b):
    return jnp.dot(a, b, preferred_element_type=F32)


def fold(value):
    return jnp.sum(value.reshape(-1, 8, 128), axis=0)


def total(value):
    return jnp.sum(jnp.sum(value, axis=0, keepdims=True), axis=1, keepdims=True)


def kernel(sizes, *refs):
    (x_hbm, b_hbm, diag_hbm, fine_hbm, coeff_hbm, f_hbm, v_hbm, lt_hbm, s_hbm, fo_hbm, xo_hbm) = refs[:11]
    (xn, bn, dg, fi, co, fb, vb, ltb, sf, X, PR, R0, P0, W1, T, GH, GL, SH, SL, LF, FN, BASE, ON, FO, XO,
     gx, gy, gz, ux, uy, uz, cx, cy, cz, zs, hx, hy, hz, own, ra, own_b, rb, own_c, rc,
     load_sem, out_sem, send_sem, recv_sem) = refs[11:]
    names = ("gx", "gy", "gz")
    me = [lax.axis_index(n) for n in names]
    up = [lax.rem(m + 1, n) for m, n in zip(me, sizes)]
    down = [lax.rem(m + n - 1, n) for m, n in zip(me, sizes)]
    has_up = [m < n - 1 for m, n in zip(me, sizes)]
    has_down = [m > 0 for m in me]

    loads = [
        pltpu.make_async_copy(src, dst, load_sem.at[k])
        for k, (src, dst) in enumerate(
            [(x_hbm, xn), (s_hbm, sf), (fine_hbm, fi), (coeff_hbm, co), (diag_hbm, dg), (b_hbm, bn),
             (f_hbm, fb), (v_hbm, vb), (lt_hbm, ltb)]
        )
    ]
    for copy in loads:
        copy.start()

    barrier = pltpu.get_barrier_semaphore()
    partners = 0
    for axis, (name, n) in enumerate(zip(names, sizes)):
        for k in range(1, n):
            pl.semaphore_signal(barrier, inc=1, device_id={name: lax.rem(me[axis] + k, n)}, device_id_type=MESH)
            partners += 1

    counter = [0]

    def send(src, dst, name, target):
        k = counter[0]
        counter[0] += 1
        copy = pltpu.make_async_remote_copy(
            src_ref=src, dst_ref=dst, send_sem=send_sem.at[k], recv_sem=recv_sem.at[k],
            device_id={name: target}, device_id_type=MESH,
        )
        copy.start()
        return copy

    lane = lax.broadcasted_iota(jnp.int32, (FD, EZ), 1)
    cells = [(i, j) for i in range(EX) for j in range(EY)]

    def keep(flag, value):
        return jnp.where(flag, value, 0.0)

    def pack(pieces, at):
        out = jnp.zeros((FD, EZ), F32)
        for n, piece in enumerate(pieces):
            out = jnp.where(lane == n, pltpu.roll(piece, (n - at) % EZ, 1), out)
        return out

    def unpack(packed, n, at):
        return pltpu.roll(packed, (at - n) % EZ, 1)

    def faces(v, k, i, j):
        n = i * EY + j
        z = v[i, j, 64:96, :]
        return [
            v[i, j, 0:32, :],
            v[i + 1, j, 0:32, :] if i + 1 < EX else hx[k, j],
            v[i, j, 32:64, :],
            v[i, j + 1, 32:64, :] if j + 1 < EY else hy[k, i],
            z,
            jnp.where(lane == EZ - 1, unpack(hz[k], n, EZ - 1), pltpu.roll(z, EZ - 1, 1)),
        ]

    def apply(v, k):
        for n, (i, j) in enumerate(cells):
            for at, block in enumerate(faces(v, k, i, j)):
                high = block.astype(BF16)
                low = (block - high.astype(F32)).astype(BF16)
                GH[32 * at : 32 * at + 32, EZ * n : EZ * n + EZ] = high
                GL[32 * at : 32 * at + 32, EZ * n : EZ * n + EZ] = low
        for n in range(0, CELLS, 2):
            cols = slice(EZ * n, EZ * n + 2 * EZ)
            high = GH[:, cols]
            product = dot(SH[...], high) + (dot(SH[...], GL[:, cols]) + dot(SL[...], high))
            for m in range(2):
                T[n + m] = product[:, EZ * m : EZ * m + EZ] * weight(n + m)

    def weight(n):
        return fi[n : n + 1, :].astype(F32) * co[n : n + 1, :]

    def gathered(i, j):
        n = i * EY + j
        along_x, along_y = T[n, 0:32, :], T[n, 64:96, :]
        if i > 0:
            along_x = along_x + T[n - EY, 32:64, :]
        if j > 0:
            along_y = along_y + T[n - 1, 96:128, :]
        along_z = T[n, 128:160, :] + jnp.where(lane == 0, 0.0, pltpu.roll(T[n, 160:192, :], 1, 1))
        return [along_x, along_y, along_z]

    def upper(i_or_j, axis):
        if axis == 0:
            return T[(EX - 1) * EY + i_or_j, 32:64, :]
        return T[i_or_j * EY + EY - 1, 96:128, :]

    def upper_z():
        return pack([T[n, 160:192, :] for n in range(CELLS)], EZ - 1)

    def diag(a, n):
        return dg[a * CELLS + n : a * CELLS + n + 1, :]

    def exchange(k, p):
        out = [send(p.at[0, :, 0:32, :], gx.at[k], "gx", down[0])]
        if k > 0:
            for j in range(EY):
                cx[k - 1, j] = upper(j, 0)
            out.append(send(cx.at[k - 1], ux.at[k - 1], "gx", up[0]))
        out.append(send(p.at[:, 0, 32:64, :], gy.at[k], "gy", down[1]))
        if k > 0:
            for i in range(EX):
                cy[k - 1, i] = upper(i, 1)
            out.append(send(cy.at[k - 1], uy.at[k - 1], "gy", up[1]))
        zs[k] = pack([p[i, j, 64:96, :] for i, j in cells], 0)
        out.append(send(zs.at[k], gz.at[k], "gz", down[2]))
        if k > 0:
            cz[k - 1] = upper_z()
            out.append(send(cz.at[k - 1], uz.at[k - 1], "gz", up[2]))
        return out

    def ghosts(k, sign):
        for j in range(EY):
            hx[k, j] = keep(has_up[0], gx[k, j] + sign * cx[k - 1, j] if k > 0 else gx[k, j])
        for i in range(EX):
            hy[k, i] = keep(has_up[1], gy[k, i] + sign * cy[k - 1, i] if k > 0 else gy[k, i])
        hz[k] = keep(has_up[2], gz[k] + sign * cz[k - 1] if k > 0 else gz[k])

    def complete(p, out, k, sign):
        for n, (i, j) in enumerate(cells):
            along_x, along_y, along_z = p[i, j, 0:32, :], p[i, j, 32:64, :], p[i, j, 64:96, :]
            if i == 0:
                along_x = along_x + sign * keep(has_down[0], ux[k - 1, j])
            if j == 0:
                along_y = along_y + sign * keep(has_down[1], uy[k - 1, i])
            below = jnp.where(lane == 0, unpack(uz[k - 1], n, 0), 0.0)
            along_z = along_z + sign * keep(has_down[2], below)
            out[i, j, 0:32, :] = along_x
            out[i, j, 32:64, :] = along_y
            out[i, j, 64:96, :] = along_z

    loads[0].wait()
    for n, (i, j) in enumerate(cells):
        X[i, j] = xn[pl.ds(n, 96, stride=CELLS), :]
    pl.semaphore_wait(barrier, partners)
    copies = exchange(0, X)
    loads[1].wait()
    s = sf[...]
    high = s.astype(BF16)
    SH[...] = high
    SL[...] = (s - high.astype(F32)).astype(BF16)
    loads[2].wait()
    loads[3].wait()
    loads[4].wait()
    loads[5].wait()
    loads[6].wait()
    for n in range(0, 3072, 128):
        FN[n : n + 128, :] = fb[n : n + 128, :].astype(F32)
    for copy in copies:
        copy.wait()
    ghosts(0, 0.0)

    apply(X, 0)
    for n, (i, j) in enumerate(cells):
        parts = gathered(i, j)
        for a in range(3):
            load = bn[pl.ds(a * FD * CELLS + n, FD, stride=CELLS), :]
            PR[i, j, 32 * a : 32 * a + 32, :] = load - diag(a, n) * X[i, j, 32 * a : 32 * a + 32, :] - parts[a]
    copies = exchange(1, PR)

    def volume(n):
        pair = [FN[pl.ds(n + m, 384, stride=CELLS), :] for m in range(2)]
        moved = dot(vb[...], jnp.concatenate([p.astype(BF16) for p in pair], axis=1))
        for m in range(2):
            coarse = 1.0 - fi[n + m : n + m + 1, :].astype(F32)
            BASE[n + m] = pair[m] + TIME_STEP * (coarse * moved[:, EZ * m : EZ * m + EZ])

    loads[7].wait()
    volume(0)
    volume(2)
    for copy in copies:
        copy.wait()
    ghosts(1, -1.0)
    complete(PR, R0, 1, -1.0)

    apply(R0, 1)
    for n, (i, j) in enumerate(cells):
        parts = gathered(i, j)
        for a in range(3):
            at = slice(32 * a, 32 * a + 32)
            P0[i, j, at, :] = diag(a, n) * R0[i, j, at, :] + parts[a]
    copies = exchange(2, P0)
    zero = jnp.zeros((8, EZ), F32)

    def over_ghosts(value):
        out = zero
        for j in range(EY):
            out = out + fold(value(hx[1, j], hx[2, j], cx[1, j], upper(j, 0)))
        for i in range(EX):
            out = out + fold(value(hy[1, i], hy[2, i], cy[1, i], upper(i, 1)))
        return out

    sum_a, sum_e00 = zero, zero
    for i, j in cells:
        r = R0[i, j]
        sum_a = sum_a + fold(r * r)
        sum_e00 = sum_e00 + fold(r * P0[i, j])
    sum_e00 = sum_e00 + over_ghosts(lambda r, w, c0, c1: r * c0) + fold(hz[1] * cz[1])
    a = total(sum_a)
    e00 = total(sum_e00)
    shift = jnp.where(a > 0.0, e00 / jnp.where(a > 0.0, a, 1.0), 0.0)
    volume(4)
    volume(6)
    loads[8].wait()
    LF[...] = ltb[...].astype(F32).T.astype(BF16)
    for copy in copies:
        copy.wait()
    ghosts(2, 1.0)
    complete(P0, W1, 2, 1.0)

    apply(W1, 2)
    sum_b, sum_c, sum_e01, sum_e11 = zero, zero, zero, zero
    for n, (i, j) in enumerate(cells):
        parts = gathered(i, j)
        for k in range(3):
            at = slice(32 * k, 32 * k + 32)
            r, w, p = R0[i, j, at, :], W1[i, j, at, :], P0[i, j, at, :]
            q = w - shift * r
            sum_b = sum_b + fold(r * q)
            sum_c = sum_c + fold(q * q)
            sum_e01 = sum_e01 + fold(q * p)
            sum_e11 = sum_e11 + fold(q * (diag(k, n) * w + parts[k] - shift * p))
    top = upper_z()
    q = hz[2] - shift * hz[1]
    sum_e01 = sum_e01 + fold(q * cz[1]) + over_ghosts(lambda r, w, c0, c1: (w - shift * r) * c0)
    sum_e11 = sum_e11 + fold(q * (top - shift * cz[1]))
    sum_e11 = sum_e11 + over_ghosts(lambda r, w, c0, c1: (w - shift * r) * (c1 - shift * c0))
    row = lax.broadcasted_iota(jnp.int32, (8, EZ), 0)
    column = lax.broadcasted_iota(jnp.int32, (8, EZ), 1)
    tile = zero
    for n, value in enumerate([shift, a, total(sum_b), total(sum_c), e00, total(sum_e01), total(sum_e11)]):
        tile = jnp.where(row == n, value, tile)
    own[...] = jnp.where(column == me[0] + sizes[0] * me[1], tile, 0.0)

    def gather(axis, source, landing):
        n = sizes[axis]
        made = [
            send(source, landing.at[k - 1], names[axis], lax.rem(me[axis] + k, n)) for k in range(1, n)
        ]
        for copy in made:
            copy.wait()

    gather(0, own, ra)
    tile = own[...]
    for k in range(sizes[0] - 1):
        tile = tile + ra[k]
    own_b[...] = tile
    gather(1, own_b, rb)
    for k in range(sizes[1] - 1):
        tile = tile + rb[k]
    own_c[...] = tile
    gather(2, own_c, rc)
    tiles = [tile] + [rc[k] for k in range(sizes[2] - 1)]

    def summed(value):
        out = value(tiles[0])
        for t in tiles[1:]:
            out = out + value(t)
        return jnp.sum(out, axis=1, keepdims=True)

    norm0 = summed(lambda t: t[1:2])
    alpha0 = norm0 / summed(lambda t: t[4:5])

    def norm1_of(t):
        f = 1.0 - alpha0 * t[0:1]
        return f * f * t[1:2] - 2.0 * alpha0 * f * t[2:3] + alpha0 * alpha0 * t[3:4]

    norm1 = summed(norm1_of)
    beta = norm1 / norm0

    def energy_of(t):
        f = 1.0 + beta - alpha0 * t[0:1]
        return f * f * t[4:5] - 2.0 * alpha0 * f * t[5:6] + alpha0 * alpha0 * t[6:7]

    alpha1 = norm1 / summed(energy_of)
    on_r = alpha0 + alpha1 * (1.0 + beta)
    on_w = -alpha1 * alpha0

    for n, (i, j) in enumerate(cells):
        new = X[i, j] + on_r * R0[i, j] + on_w * W1[i, j]
        R0[i, j] = new
        XO[pl.ds(n, 96, stride=CELLS), :] = new
    out_x = pltpu.make_async_copy(XO, xo_hbm, out_sem.at[0])
    out_x.start()
    for j in range(EY):
        hx[1, j] = hx[0, j] + on_r * hx[1, j] + on_w * hx[2, j]
    for i in range(EX):
        hy[1, i] = hy[0, i] + on_r * hy[1, i] + on_w * hy[2, i]
    hz[1] = hz[0] + on_r * hz[1] + on_w * hz[2]
    for n, (i, j) in enumerate(cells):
        fine = fi[n : n + 1, :] > 0
        for at, (new, old) in enumerate(zip(faces(R0, 1, i, j), faces(X, 0, i, j))):
            GH[32 * at : 32 * at + 32, EZ * n : EZ * n + EZ] = jnp.where(fine, new, old).astype(BF16)
    for n in range(0, CELLS, 2):
        lifted = dot(LF[...], GH[:, EZ * n : EZ * n + 2 * EZ])
        for m in range(2):
            ON[pl.ds(n + m, 384, stride=CELLS), :] = BASE[n + m] + TIME_STEP * lifted[:, EZ * m : EZ * m + EZ]
    for n in range(0, 3072, 128):
        FO[n : n + 128, :] = ON[n : n + 128, :].astype(BF16)
    out_f = pltpu.make_async_copy(FO, fo_hbm, out_sem.at[1])
    out_f.start()
    out_x.wait()
    out_f.wait()


def solution(mesh):
    sizes = tuple(mesh.shape[n] for n in ("gx", "gy", "gz"))

    def body(fields, trace_old, face_load, face_diag, fine_flag, coeff, volume_op, lift_op, schur_op):
        vmem = pltpu.VMEM
        field = (EX, EY, 96, EZ)
        copies = 3 + 6 + 6 + sum(sizes) - 3
        scratch = [
            vmem((768, EZ), F32), vmem((768, EZ), F32), vmem((24, EZ), F32), vmem((8, EZ), jnp.int32),
            vmem((8, EZ), F32), vmem((3072, EZ), BF16), vmem((384, 384), BF16), vmem((192, 384), BF16),
            vmem((192, 192), F32),
            vmem(field, F32), vmem(field, F32), vmem(field, F32), vmem(field, F32), vmem(field, F32),
            vmem((CELLS, 192, EZ), F32), vmem((192, CELLS * EZ), BF16), vmem((192, CELLS * EZ), BF16),
            vmem((192, 192), BF16), vmem((192, 192), BF16), vmem((384, 192), BF16),
            vmem((3072, EZ), F32), vmem((CELLS, 384, EZ), F32), vmem((3072, EZ), F32), vmem((3072, EZ), BF16),
            vmem((768, EZ), F32),
            vmem((3, EY, FD, EZ), F32), vmem((3, EX, FD, EZ), F32), vmem((3, FD, EZ), F32),
            vmem((2, EY, FD, EZ), F32), vmem((2, EX, FD, EZ), F32), vmem((2, FD, EZ), F32),
            vmem((2, EY, FD, EZ), F32), vmem((2, EX, FD, EZ), F32), vmem((2, FD, EZ), F32),
            vmem((3, FD, EZ), F32),
            vmem((3, EY, FD, EZ), F32), vmem((3, EX, FD, EZ), F32), vmem((3, FD, EZ), F32),
            vmem((8, EZ), F32), vmem((sizes[0] - 1, 8, EZ), F32), vmem((8, EZ), F32),
            vmem((sizes[1] - 1, 8, EZ), F32), vmem((8, EZ), F32), vmem((sizes[2] - 1, 8, EZ), F32),
            pltpu.SemaphoreType.DMA((9,)), pltpu.SemaphoreType.DMA((2,)),
            pltpu.SemaphoreType.DMA((copies,)), pltpu.SemaphoreType.DMA((copies,)),
        ]
        out_f, out_x = pl.pallas_call(
            functools.partial(kernel, sizes),
            out_shape=(jax.ShapeDtypeStruct((3072, EZ), BF16), jax.ShapeDtypeStruct((768, EZ), F32)),
            in_specs=[pl.BlockSpec(memory_space=pl.ANY)] * 9,
            out_specs=(pl.BlockSpec(memory_space=pl.ANY),) * 2,
            scratch_shapes=scratch,
            compiler_params=pltpu.CompilerParams(
                collective_id=0, has_side_effects=True, vmem_limit_bytes=40 * 1024 * 1024
            ),
            name="step",
        )(
            trace_old.reshape(768, EZ), face_load.reshape(768, EZ), face_diag.reshape(24, EZ),
            fine_flag.reshape(8, EZ), coeff.reshape(8, EZ), fields.reshape(3072, EZ), volume_op, lift_op.T, schur_op,
        )
        return out_f.reshape(fields.shape), out_x.reshape(trace_old.shape)

    return jax.shard_map(
        body,
        mesh=mesh,
        in_specs=(
            P(None, "gx", "gy", "gz"),
            P(None, None, "gx", "gy", "gz"),
            P(None, None, "gx", "gy", "gz"),
            P(None, "gx", "gy", "gz"),
            P("gx", "gy", "gz"),
            P("gx", "gy", "gz"),
            P(),
            P(),
            P(),
        ),
        out_specs=(P(None, "gx", "gy", "gz"), P(None, None, "gx", "gy", "gz")),
        check_vma=False,
    )
```

time: 333 us -> 46.5 us (0.14)
  the two profiles are of different devices: /device:TPU:8 before, /device:TPU:1 now
where the time goes in v1:
time: 46.5 us; the launch traced here: 46.1 us
  Pallas kernels  35.8 us (77%)
  local copies, waits for them, and re-layouts  9.62 us (21%)
  between operations  0.66 us (1%)
    pallas_call x1, Pallas kernels, body(): pl.pallas_call(functools.partial(kernel, sizes), out_shape=(jax.ShapeDtyp...  35.8 us
    unnamed x20, local copies, waits for them, and re-layouts  9.62 us

profile of v1, /device:TPU:1, one launch (start us, length us, event | category | flops | bytes accessed | tf_op | source)
XLA Modules:
  0.0 46.1 jit_solution(6464018249042392924)
XLA Ops:
  0.6 0.0 copy-start.6
  0.6 0.7 %copy-done.6 = f32[3,2,4,128]{3,2,1,0:T(4,128)S(1)} copy-done((f32[3,2,4,128]{3,2,1,0:T(4,128)S(1)}, f32[3,2,4,128]{3,2,1,0:T(4,128)}, u32[]{:S(2)}) %copy-start.6) | copy-done | bytes 12312
  1.3 0.0 copy-start
  1.3 1.1 %copy-done = bf16[384,2,4,128]{3,2,1,0:T(4,128)(2,1)S(1)} copy-done((bf16[384,2,4,128]{3,2,1,0:T(4,128)(2,1)S(1)}, bf16[384,2,4,128]{3,2,1,0:T(4,128)(2,1)}, u32[]{:S(2)}) %copy-start) | copy-done | bytes 786456
  2.5 0.0 copy-start.1
  2.5 1.0 %copy-done.1 = f32[3,32,2,4,128]{4,3,2,1,0:T(4,128)S(1)} copy-done((f32[3,32,2,4,128]{4,3,2,1,0:T(4,128)S(1)}, f32[3,32,2,4,128]{4,3,2,1,0:T(4,128)}, u32[]{:S(2)}) %copy-start.1) | copy-done | bytes 393240
  3.5 0.0 copy-start.2
  3.5 1.0 %copy-done.2 = f32[3,32,2,4,128]{4,3,2,1,0:T(4,128)S(1)} copy-done((f32[3,32,2,4,128]{4,3,2,1,0:T(4,128)S(1)}, f32[3,32,2,4,128]{4,3,2,1,0:T(4,128)}, u32[]{:S(2)}) %copy-start.2) | copy-done | bytes 393240
  4.5 0.0 copy-start.3
  4.5 1.0 %copy-done.3 = bf16[384,384]{1,0:T(8,128)(2,1)S(1)} copy-done((bf16[384,384]{1,0:T(8,128)(2,1)S(1)}, bf16[384,384]{1,0:T(8,128)(2,1)}, u32[]{:S(2)}) %copy-start.3) | copy-done | bytes 294936
  5.4 0.0 copy-start.4
  5.4 0.9 %copy-done.4 = f32[192,192]{1,0:T(8,128)S(1)} copy-done((f32[192,192]{1,0:T(8,128)S(1)}, f32[192,192]{1,0:T(8,128)}, u32[]{:S(2)}) %copy-start.4) | copy-done | bytes 147480
  6.4 0.0 copy-start.5
  6.4 0.9 %copy-done.5 = bf16[384,192]{0,1:T(8,128)(2,1)S(1)} copy-done((bf16[384,192]{0,1:T(8,128)(2,1)S(1)}, bf16[384,192]{0,1:T(8,128)(2,1)}, u32[]{:S(2)}) %copy-start.5) | copy-done | bytes 147480
  7.3 0.0 copy-start.7
  7.3 0.7 %copy-done.7 = s32[2,4,128]{2,1,0:T(4,128)S(1)} copy-done((s32[2,4,128]{2,1,0:T(4,128)S(1)}, s32[2,4,128]{2,1,0:T(4,128)}, u32[]{:S(2)}) %copy-start.7) | copy-done | bytes 4120
  8.0 0.0 copy-start.8
  8.0 0.7 %copy-done.8 = f32[2,4,128]{2,1,0:T(4,128)S(1)} copy-done((f32[2,4,128]{2,1,0:T(4,128)S(1)}, f32[2,4,128]{2,1,0:T(4,128)}, u32[]{:S(2)}) %copy-start.8) | copy-done | bytes 4120
  8.6 35.8 %step.1 = (bf16[3072,128]{1,0:T(8,128)(2,1)S(1)}, f32[768,128]{1,0:T(8,128)S(1)}) custom-call(f32[768,128]{1,0:T(8,128)S(1)} %bitcast.12, f32[768,128]{1,0:T(8,128)S(1)} %bitcast.13, f32[24,128]{1,0:T(8,128)S(1)} %bitcast.15, s32[8,128]{1,0:T(8,128)S(1)} %bitcast.16, f32[8,128]{1,0:T(8,128)S(1)} %bitcast.17, bf16[3072,128]{1,0:T(8,128)(2,1)S(1)} %bitcast.9, ...), custom_call_target="tpu_custom_call" | custom-call | tf_op jit(solution)/shard_map/step/pallas_call | solution.py:374
  44.4 0.9 %copy.13 = bf16[384,2,4,128]{3,2,1,0:T(4,128)(2,1)} copy(bf16[384,2,4,128]{3,2,1,0:T(4,128)(2,1)S(1)} %bitcast.10) | data formatting | bytes 1572864
  45.3 0.7 %copy.14 = f32[3,32,2,4,128]{4,3,2,1,0:T(4,128)} copy(f32[3,32,2,4,128]{4,3,2,1,0:T(4,128)S(1)} %bitcast.11) | data formatting | bytes 786432
Async XLA Ops:
  0.6 0.7 %copy-start.6 = (f32[3,2,4,128]{3,2,1,0:T(4,128)S(1)}, f32[3,2,4,128]{3,2,1,0:T(4,128)}, u32[]{:S(2)}) copy-start(f32[3,2,4,128]{3,2,1,0:T(4,128)} %param.12) | copy-start | bytes 36868
  1.3 1.1 %copy-start = (bf16[384,2,4,128]{3,2,1,0:T(4,128)(2,1)S(1)}, bf16[384,2,4,128]{3,2,1,0:T(4,128)(2,1)}, u32[]{:S(2)}) copy-start(bf16[384,2,4,128]{3,2,1,0:T(4,128)(2,1)} %param.9) | copy-start | bytes 2359300
  2.5 1.0 %copy-start.1 = (f32[3,32,2,4,128]{4,3,2,1,0:T(4,128)S(1)}, f32[3,32,2,4,128]{4,3,2,1,0:T(4,128)}, u32[]{:S(2)}) copy-start(f32[3,32,2,4,128]{4,3,2,1,0:T(4,128)} %param.10) | copy-start | bytes 1179652
  3.5 1.0 %copy-start.2 = (f32[3,32,2,4,128]{4,3,2,1,0:T(4,128)S(1)}, f32[3,32,2,4,128]{4,3,2,1,0:T(4,128)}, u32[]{:S(2)}) copy-start(f32[3,32,2,4,128]{4,3,2,1,0:T(4,128)} %param.11) | copy-start | bytes 1179652
  4.5 1.0 %copy-start.3 = (bf16[384,384]{1,0:T(8,128)(2,1)S(1)}, bf16[384,384]{1,0:T(8,128)(2,1)}, u32[]{:S(2)}) copy-start(bf16[384,384]{1,0:T(8,128)(2,1)} %refs_6_.1) | copy-start | bytes 884740
  5.4 0.9 %copy-start.4 = (f32[192,192]{1,0:T(8,128)S(1)}, f32[192,192]{1,0:T(8,128)}, u32[]{:S(2)}) copy-start(f32[192,192]{1,0:T(8,128)} %refs_8_.1) | copy-start | bytes 442372
  6.4 0.9 %copy-start.5 = (bf16[384,192]{0,1:T(8,128)(2,1)S(1)}, bf16[384,192]{0,1:T(8,128)(2,1)}, u32[]{:S(2)}) copy-start(bf16[384,192]{0,1:T(8,128)(2,1)} %param.16) | copy-start | bytes 442372
  7.3 0.7 %copy-start.7 = (s32[2,4,128]{2,1,0:T(4,128)S(1)}, s32[2,4,128]{2,1,0:T(4,128)}, u32[]{:S(2)}) copy-start(s32[2,4,128]{2,1,0:T(4,128)} %param.13) | copy-start | bytes 12292
  8.0 0.7 %copy-start.8 = (f32[2,4,128]{2,1,0:T(4,128)S(1)}, f32[2,4,128]{2,1,0:T(4,128)}, u32[]{:S(2)}) copy-start(f32[2,4,128]{2,1,0:T(4,128)} %param.14) | copy-start | bytes 12292

commit v2 on v1

--- a/solution.py
+++ b/solution.py
@@ -27,11 +27,21 @@
     return jnp.sum(jnp.sum(value, axis=0, keepdims=True), axis=1, keepdims=True)
 
 
+def across(sizes):
+    steps = [(y, z) for y in range(sizes[0] // 2) for z in range(sizes[2]) if y or z]
+    return sorted(steps, key=lambda s: -min(s[0], sizes[0] // 2 - s[0]) - min(s[1], sizes[2] - s[1]))
+
+
+def along(sizes):
+    steps = [(c, z) for z in range(sizes[1]) for c in range(2) if c or z]
+    return sorted(steps, key=lambda s: -min(s[1], sizes[1] - s[1]) - 0.5 * s[0])
+
+
 def kernel(sizes, *refs):
-    (x_hbm, b_hbm, diag_hbm, fine_hbm, coeff_hbm, f_hbm, v_hbm, lt_hbm, s_hbm, fo_hbm, xo_hbm) = refs[:11]
-    (xn, bn, dg, fi, co, fb, vb, ltb, sf, X, PR, R0, P0, W1, T, GH, GL, SH, SL, LF, FN, BASE, ON, FO, XO,
-     gx, gy, gz, ux, uy, uz, cx, cy, cz, zs, hx, hy, hz, own, ra, own_b, rb, own_c, rc,
-     load_sem, out_sem, send_sem, recv_sem) = refs[11:]
+    (x_hbm, b_hbm, diag_hbm, fine_hbm, coeff_hbm, f_hbm, v_hbm, lt_hbm, s_hbm, FO, XO) = refs[:11]
+    (xn, bn, dg, fi, co, fb, vb, ltb, sf, X, PR, R0, P0, W1, T, GH, GL, SH, SL, LF, FN, BASE, ON,
+     gx, gy, gz, ux, uy, uz, cx, cy, cz, zs, hx, hy, hz, own, ra, own_b, rb,
+     load_sem, send_sem, recv_sem, gather_send, gather_recv, know) = refs[11:]
     names = ("gx", "gy", "gz")
     me = [lax.axis_index(n) for n in names]
     up = [lax.rem(m + 1, n) for m, n in zip(me, sizes)]
@@ -50,22 +60,32 @@
         copy.start()
 
     barrier = pltpu.get_barrier_semaphore()
-    partners = 0
-    for axis, (name, n) in enumerate(zip(names, sizes)):
-        for k in range(1, n):
-            pl.semaphore_signal(barrier, inc=1, device_id={name: lax.rem(me[axis] + k, n)}, device_id_type=MESH)
-            partners += 1
-
-    counter = [0]
+
+    def announce(sem, steps):
+        count = 0
+        for axis, step in steps:
+            n = sizes[axis]
+            if step % n:
+                target = lax.rem(me[axis] + step + n, n)
+                pl.semaphore_signal(sem, inc=1, device_id={names[axis]: target}, device_id_type=MESH)
+                count += 1
+        return count
+
+    near = [(axis, step) for axis in range(3) for step in (1, -1)]
+    partners = announce(barrier, near)
+    core = lax.rem(me[0], 2)
+    other_core = me[0] + 1 - 2 * core
+
+    started = []
 
     def send(src, dst, name, target):
-        k = counter[0]
-        counter[0] += 1
+        k = len(started)
         copy = pltpu.make_async_remote_copy(
             src_ref=src, dst_ref=dst, send_sem=send_sem.at[k], recv_sem=recv_sem.at[k],
             device_id={name: target}, device_id_type=MESH,
         )
         copy.start()
+        started.append(copy)
         return copy
 
     lane = lax.broadcasted_iota(jnp.int32, (FD, EZ), 1)
@@ -175,6 +195,7 @@
     for n, (i, j) in enumerate(cells):
         X[i, j] = xn[pl.ds(n, 96, stride=CELLS), :]
     pl.semaphore_wait(barrier, partners)
+    known_1 = announce(know.at[0], near)
     copies = exchange(0, X)
     loads[1].wait()
     s = sf[...]
@@ -189,7 +210,9 @@
     for n in range(0, 3072, 128):
         FN[n : n + 128, :] = fb[n : n + 128, :].astype(F32)
     for copy in copies:
-        copy.wait()
+        copy.wait_recv()
+    pl.semaphore_wait(know.at[0], known_1)
+    known_2 = announce(know.at[1], [(axis, step) for axis in range(2) for step in (2, -2)])
     ghosts(0, 0.0)
 
     apply(X, 0)
@@ -211,7 +234,11 @@
     volume(0)
     volume(2)
     for copy in copies:
-        copy.wait()
+        copy.wait_recv()
+    if known_2:
+        pl.semaphore_wait(know.at[1], known_2)
+    known_3 = 1 + announce(know.at[2], [(2, 1), (2, -1), (2, 2)])
+    pl.semaphore_signal(know.at[2], inc=1, device_id={"gx": other_core}, device_id_type=MESH)
     ghosts(1, -1.0)
     complete(PR, R0, 1, -1.0)
 
@@ -246,7 +273,8 @@
     loads[8].wait()
     LF[...] = ltb[...].astype(F32).T.astype(BF16)
     for copy in copies:
-        copy.wait()
+        copy.wait_recv()
+    pl.semaphore_wait(know.at[2], known_3)
     ghosts(2, 1.0)
     complete(P0, W1, 2, 1.0)
 
@@ -272,33 +300,35 @@
     tile = zero
     for n, value in enumerate([shift, a, total(sum_b), total(sum_c), e00, total(sum_e01), total(sum_e11)]):
         tile = jnp.where(row == n, value, tile)
-    own[...] = jnp.where(column == me[0] + sizes[0] * me[1], tile, 0.0)
-
-    def gather(axis, source, landing):
-        n = sizes[axis]
-        made = [
-            send(source, landing.at[k - 1], names[axis], lax.rem(me[axis] + k, n)) for k in range(1, n)
-        ]
-        for copy in made:
-            copy.wait()
-
-    gather(0, own, ra)
-    tile = own[...]
-    for k in range(sizes[0] - 1):
-        tile = tile + ra[k]
-    own_b[...] = tile
-    gather(1, own_b, rb)
-    for k in range(sizes[1] - 1):
-        tile = tile + rb[k]
-    own_c[...] = tile
-    gather(2, own_c, rc)
-    tiles = [tile] + [rc[k] for k in range(sizes[2] - 1)]
+    planes, layers = sizes[0] // 2, max(sizes[1] // 2, 1)
+    group = planes * sizes[2]
+    place = lax.div(me[0], 2) + planes * me[2] + group * (core + 2 * lax.rem(me[1], layers))
+    own[...] = jnp.where(column == place, tile, 0.0)
+
+    def gather(k, source, landing, targets):
+        for n, target in enumerate(targets):
+            pltpu.make_async_remote_copy(
+                src_ref=source, dst_ref=landing.at[n], send_sem=gather_send.at[k], recv_sem=gather_recv.at[k],
+                device_id=target, device_id_type=MESH,
+            ).start()
+        out = source[...]
+        pltpu.make_async_copy(landing, landing, gather_recv.at[k]).wait()
+        for n in range(len(targets)):
+            out = out + landing[n]
+        return out
+
+    tile = gather(0, own, ra, [
+        {"gx": lax.rem(me[0] + 2 * y, sizes[0]), "gz": lax.rem(me[2] + z, sizes[2])} for y, z in across(sizes)
+    ])
+    low = me[1] < layers
+    own_b[0:8, :] = keep(low, tile)
+    own_b[8:16, :] = keep(jnp.logical_not(low), tile)
+    tile = gather(1, own_b, rb, [
+        {"gx": other_core if c else me[0], "gy": lax.rem(me[1] + z, sizes[1])} for c, z in along(sizes)
+    ])
 
     def summed(value):
-        out = value(tiles[0])
-        for t in tiles[1:]:
-            out = out + value(t)
-        return jnp.sum(out, axis=1, keepdims=True)
+        return jnp.sum(value(tile[0:8]) + value(tile[8:16]), axis=1, keepdims=True)
 
     norm0 = summed(lambda t: t[1:2])
     alpha0 = norm0 / summed(lambda t: t[4:5])
@@ -322,8 +352,6 @@
         new = X[i, j] + on_r * R0[i, j] + on_w * W1[i, j]
         R0[i, j] = new
         XO[pl.ds(n, 96, stride=CELLS), :] = new
-    out_x = pltpu.make_async_copy(XO, xo_hbm, out_sem.at[0])
-    out_x.start()
     for j in range(EY):
         hx[1, j] = hx[0, j] + on_r * hx[1, j] + on_w * hx[2, j]
     for i in range(EX):
@@ -339,10 +367,10 @@
             ON[pl.ds(n + m, 384, stride=CELLS), :] = BASE[n + m] + TIME_STEP * lifted[:, EZ * m : EZ * m + EZ]
     for n in range(0, 3072, 128):
         FO[n : n + 128, :] = ON[n : n + 128, :].astype(BF16)
-    out_f = pltpu.make_async_copy(FO, fo_hbm, out_sem.at[1])
-    out_f.start()
-    out_x.wait()
-    out_f.wait()
+    for copy in started:
+        copy.wait_send()
+    pltpu.make_async_copy(ra, ra, gather_send.at[0]).wait()
+    pltpu.make_async_copy(rb, rb, gather_send.at[1]).wait()
 
 
 def solution(mesh):
@@ -351,7 +379,8 @@
     def body(fields, trace_old, face_load, face_diag, fine_flag, coeff, volume_op, lift_op, schur_op):
         vmem = pltpu.VMEM
         field = (EX, EY, 96, EZ)
-        copies = 3 + 6 + 6 + sum(sizes) - 3
+        copies = 3 + 6 + 6
+        group, column = len(across(sizes)), len(along(sizes))
         scratch = [
             vmem((768, EZ), F32), vmem((768, EZ), F32), vmem((24, EZ), F32), vmem((8, EZ), jnp.int32),
             vmem((8, EZ), F32), vmem((3072, EZ), BF16), vmem((384, 384), BF16), vmem((192, 384), BF16),
@@ -359,31 +388,36 @@
             vmem(field, F32), vmem(field, F32), vmem(field, F32), vmem(field, F32), vmem(field, F32),
             vmem((CELLS, 192, EZ), F32), vmem((192, CELLS * EZ), BF16), vmem((192, CELLS * EZ), BF16),
             vmem((192, 192), BF16), vmem((192, 192), BF16), vmem((384, 192), BF16),
-            vmem((3072, EZ), F32), vmem((CELLS, 384, EZ), F32), vmem((3072, EZ), F32), vmem((3072, EZ), BF16),
-            vmem((768, EZ), F32),
+            vmem((3072, EZ), F32), vmem((CELLS, 384, EZ), F32), vmem((3072, EZ), F32),
             vmem((3, EY, FD, EZ), F32), vmem((3, EX, FD, EZ), F32), vmem((3, FD, EZ), F32),
             vmem((2, EY, FD, EZ), F32), vmem((2, EX, FD, EZ), F32), vmem((2, FD, EZ), F32),
             vmem((2, EY, FD, EZ), F32), vmem((2, EX, FD, EZ), F32), vmem((2, FD, EZ), F32),
             vmem((3, FD, EZ), F32),
             vmem((3, EY, FD, EZ), F32), vmem((3, EX, FD, EZ), F32), vmem((3, FD, EZ), F32),
-            vmem((8, EZ), F32), vmem((sizes[0] - 1, 8, EZ), F32), vmem((8, EZ), F32),
-            vmem((sizes[1] - 1, 8, EZ), F32), vmem((8, EZ), F32), vmem((sizes[2] - 1, 8, EZ), F32),
-            pltpu.SemaphoreType.DMA((9,)), pltpu.SemaphoreType.DMA((2,)),
+            vmem((8, EZ), F32), vmem((group, 8, EZ), F32), vmem((16, EZ), F32), vmem((column, 16, EZ), F32),
+            pltpu.SemaphoreType.DMA((9,)),
             pltpu.SemaphoreType.DMA((copies,)), pltpu.SemaphoreType.DMA((copies,)),
+            pltpu.SemaphoreType.DMA((2,)), pltpu.SemaphoreType.DMA((2,)), pltpu.SemaphoreType.REGULAR((3,)),
         ]
         out_f, out_x = pl.pallas_call(
             functools.partial(kernel, sizes),
             out_shape=(jax.ShapeDtypeStruct((3072, EZ), BF16), jax.ShapeDtypeStruct((768, EZ), F32)),
-            in_specs=[pl.BlockSpec(memory_space=pl.ANY)] * 9,
-            out_specs=(pl.BlockSpec(memory_space=pl.ANY),) * 2,
+            in_specs=[pl.BlockSpec(memory_space=pltpu.HBM)] * 9,
+            out_specs=(pl.BlockSpec(memory_space=pltpu.VMEM),) * 2,
             scratch_shapes=scratch,
             compiler_params=pltpu.CompilerParams(
                 collective_id=0, has_side_effects=True, vmem_limit_bytes=40 * 1024 * 1024
             ),
             name="step",
         )(
-            trace_old.reshape(768, EZ), face_load.reshape(768, EZ), face_diag.reshape(24, EZ),
-            fine_flag.reshape(8, EZ), coeff.reshape(8, EZ), fields.reshape(3072, EZ), volume_op, lift_op.T, schur_op,
+            *(
+                pltpu.with_memory_space_constraint(value, pltpu.HBM)
+                for value in (
+                    trace_old.reshape(768, EZ), face_load.reshape(768, EZ), face_diag.reshape(24, EZ),
+                    fine_flag.reshape(8, EZ), coeff.reshape(8, EZ), fields.reshape(3072, EZ), volume_op, lift_op.T,
+                    schur_op,
+                )
+            )
         )
         return out_f.reshape(fields.shape), out_x.reshape(trace_old.shape)
 

time: 46.5 us -> 35.4 us (0.76)
  local copies, waits for them, and re-layouts: 9.62 us -> 1.63 us
  Pallas kernels: 35.8 us -> 33.1 us
    unnamed x20 -> x2, local copies, waits for them, and re-layouts: 9.62 us -> 1.63 us
    pallas_call x1, Pallas kernels: 35.8 us -> 33.1 us  [body(): pl.pallas_call(functools.partial(kernel, sizes), out_shape=(jax.ShapeDtyp...]
where the time goes in v2:
time: 35.4 us; the launch traced here: 35.3 us
  Pallas kernels  33.1 us (94%)
  local copies, waits for them, and re-layouts  1.63 us (5%)
  between operations  0.64 us (2%)
    pallas_call x1, Pallas kernels, body(): pl.pallas_call(functools.partial(kernel, sizes), out_shape=(jax.ShapeDtyp...  33.1 us
    unnamed x2, local copies, waits for them, and re-layouts  1.63 us

profile of v2, /device:TPU:1, one launch (start us, length us, event | category | flops | bytes accessed | tf_op | source)
XLA Modules:
  0.0 35.3 jit_solution(2093652951904854349)
XLA Ops:
  0.6 33.1 %step.1 = (bf16[3072,128]{1,0:T(8,128)(2,1)S(1)}, f32[768,128]{1,0:T(8,128)S(1)}) custom-call(f32[768,128]{1,0:T(8,128)} %bitcast.12, f32[768,128]{1,0:T(8,128)} %bitcast.13, f32[24,128]{1,0:T(8,128)} %bitcast.15, s32[8,128]{1,0:T(8,128)} %bitcast.16, f32[8,128]{1,0:T(8,128)} %bitcast.17, bf16[3072,128]{1,0:T(8,128)(2,1)} %bitcast.11, ...), custom_call_target="tpu_custom_call" | custom-call | tf_op jit(solution)/shard_map/step/pallas_call | solution.py:402
  33.7 0.9 %copy.13 = bf16[384,2,4,128]{3,2,1,0:T(4,128)(2,1)} copy(bf16[384,2,4,128]{3,2,1,0:T(4,128)(2,1)S(1)} %bitcast.9) | data formatting | bytes 1572864
  34.6 0.7 %copy.14 = f32[3,32,2,4,128]{4,3,2,1,0:T(4,128)} copy(f32[3,32,2,4,128]{4,3,2,1,0:T(4,128)S(1)} %bitcast.10) | data formatting | bytes 786432

commit v3 on v2

v3 whole, which is shorter than its diff:
```python
import functools

import jax
import jax.numpy as jnp
from jax import lax
from jax.experimental import pallas as pl
from jax.experimental.pallas import tpu as pltpu
from jax.sharding import PartitionSpec as P

MESH = pl.DeviceIdType.MESH
EX, EY, EZ = 2, 4, 128
CELLS = EX * EY
FD = 32
F32, BF16 = jnp.float32, jnp.bfloat16
TIME_STEP = 0.25
CHUNKS = 3


def dot(a, b):
    return jnp.dot(a, b, preferred_element_type=F32)


def fold(value):
    return jnp.sum(value.reshape(-1, 8, 128), axis=0)


def total(value):
    return jnp.sum(jnp.sum(value, axis=0, keepdims=True), axis=1, keepdims=True)


def across(sizes):
    steps = [(y, z) for y in range(sizes[0] // 2) for z in range(sizes[2]) if y or z]
    return sorted(steps, key=lambda s: -min(s[0], sizes[0] // 2 - s[0]) - min(s[1], sizes[2] - s[1]))


def along(sizes):
    steps = [(c, z) for z in range(sizes[1]) for c in range(2) if c or z]
    return sorted(steps, key=lambda s: -min(s[1], sizes[1] - s[1]) - 0.5 * s[0])


def unpack(packed, n, at):
    return pltpu.roll(packed, (at - n) % EZ, 1)


def faces_of(v, hx, hy, hz, lane, i, j):
    n = i * EY + j
    z = v[i, j, 64:96, :]
    return [
        v[i, j, 0:32, :],
        v[i + 1, j, 0:32, :] if i + 1 < EX else hx[j],
        v[i, j, 32:64, :],
        v[i, j + 1, 32:64, :] if j + 1 < EY else hy[i],
        z,
        jnp.where(lane == EZ - 1, unpack(hz[...], n, EZ - 1), pltpu.roll(z, EZ - 1, 1)),
    ]


def kernel(sizes, *refs):
    (x_hbm, b_hbm, diag_hbm, fine_hbm, coeff_hbm, f_hbm, v_hbm, lt_hbm, s_hbm) = refs[:9]
    (moments, X, R0, W1, hx, hy, hz, BASE, LF, fi) = refs[9:19]
    (xn, bn, dg, co, fb, vb, ltb, sf, PR, P0, T, GH, GL, SH, SL, FN,
     gx, gy, gz, ux, uy, uz, cx, cy, cz, zs, own, ra, own_b, rb,
     load_sem, send_sem, recv_sem, gather_send, gather_recv, know) = refs[19:]
    names = ("gx", "gy", "gz")
    me = [lax.axis_index(n) for n in names]
    up = [lax.rem(m + 1, n) for m, n in zip(me, sizes)]
    down = [lax.rem(m + n - 1, n) for m, n in zip(me, sizes)]
    has_up = [m < n - 1 for m, n in zip(me, sizes)]
    has_down = [m > 0 for m in me]

    barrier = pltpu.get_barrier_semaphore()

    def announce(sem, steps):
        count = 0
        for axis, step in steps:
            n = sizes[axis]
            if step % n:
                target = lax.rem(me[axis] + step + n, n)
                pl.semaphore_signal(sem, inc=1, device_id={names[axis]: target}, device_id_type=MESH)
                count += 1
        return count

    near = [(axis, step) for axis in range(3) for step in (1, -1)]
    partners = announce(barrier, near)
    loads = [
        pltpu.make_async_copy(src, dst, load_sem.at[k])
        for k, (src, dst) in enumerate(
            [(x_hbm.at[256 * a : 256 * a + 256, :], xn.at[256 * a : 256 * a + 256, :]) for a in range(3)]
            + [(s_hbm, sf), (fine_hbm, fi), (coeff_hbm, co), (diag_hbm, dg), (b_hbm, bn),
               (f_hbm, fb), (v_hbm, vb), (lt_hbm, ltb)]
        )
    ]
    for copy in loads:
        copy.start()
    core = lax.rem(me[0], 2)
    other_core = me[0] + 1 - 2 * core

    started = []

    def send(src, dst, name, target):
        k = len(started)
        copy = pltpu.make_async_remote_copy(
            src_ref=src, dst_ref=dst, send_sem=send_sem.at[k], recv_sem=recv_sem.at[k],
            device_id={name: target}, device_id_type=MESH,
        )
        copy.start()
        started.append(copy)
        return copy

    lane = lax.broadcasted_iota(jnp.int32, (FD, EZ), 1)
    cells = [(i, j) for i in range(EX) for j in range(EY)]

    def keep(flag, value):
        return jnp.where(flag, value, 0.0)

    def pack(pieces, at):
        out = jnp.zeros((FD, EZ), F32)
        for n, piece in enumerate(pieces):
            out = jnp.where(lane == n, pltpu.roll(piece, (n - at) % EZ, 1), out)
        return out

    def faces(v, k, i, j):
        return faces_of(v, hx.at[k], hy.at[k], hz.at[k], lane, i, j)

    def apply(v, k, half):
        for n, (i, j) in enumerate(cells):
            if i != half:
                continue
            for at, block in enumerate(faces(v, k, i, j)):
                high = block.astype(BF16)
                low = (block - high.astype(F32)).astype(BF16)
                GH[32 * at : 32 * at + 32, EZ * n : EZ * n + EZ] = high
                GL[32 * at : 32 * at + 32, EZ * n : EZ * n + EZ] = low
        for n in range(EY * half, EY * half + EY, 2):
            cols = slice(EZ * n, EZ * n + 2 * EZ)
            high = GH[:, cols]
            product = dot(SH[...], high) + (dot(SH[...], GL[:, cols]) + dot(SL[...], high))
            for m in range(2):
                T[n + m] = product[:, EZ * m : EZ * m + EZ] * weight(n + m)

    def weight(n):
        return fi[n : n + 1, :].astype(F32) * co[n : n + 1, :]

    def gathered(i, j, a):
        n = i * EY + j
        at = 64 * a
        value = T[n, at : at + 32, :]
        if a == 0 and i > 0:
            value = value + T[n - EY, at + 32 : at + 64, :]
        if a == 1 and j > 0:
            value = value + T[n - 1, at + 32 : at + 64, :]
        if a == 2:
            value = value + jnp.where(lane == 0, 0.0, pltpu.roll(T[n, at + 32 : at + 64, :], 1, 1))
        return value

    def upper(i_or_j, axis):
        if axis == 0:
            return T[(EX - 1) * EY + i_or_j, 32:64, :]
        return T[i_or_j * EY + EY - 1, 96:128, :]

    def upper_z():
        return pack([T[n, 160:192, :] for n in range(CELLS)], EZ - 1)

    def diag(a, n):
        return dg[a * CELLS + n : a * CELLS + n + 1, :]

    def old_exchange(k, p):
        return [
            send(p.at[0, :, 0:32, :], gx.at[k], "gx", down[0]),
            send(p.at[:, 0, 32:64, :], gy.at[k], "gy", down[1]),
        ]

    def round_trip(v, p, k, partial):
        out = []
        done = set()

        def put(i, j, a):
            p[i, j, 32 * a : 32 * a + 32, :] = partial(i, j, a)
            done.add((i, j, a))

        apply(v, k - 1, 0)
        for j in range(EY):
            put(0, j, 0)
        out.append(send(p.at[0, :, 0:32, :], gx.at[k], "gx", down[0]))
        apply(v, k - 1, 1)
        for j in range(EY):
            cx[k - 1, j] = upper(j, 0)
        out.append(send(cx.at[k - 1], ux.at[k - 1], "gx", up[0]))
        for i in range(EX):
            put(i, 0, 1)
        out.append(send(p.at[:, 0, 32:64, :], gy.at[k], "gy", down[1]))
        for i in range(EX):
            cy[k - 1, i] = upper(i, 1)
        out.append(send(cy.at[k - 1], uy.at[k - 1], "gy", up[1]))
        for i, j in cells:
            put(i, j, 2)
        zs[k] = pack([p[i, j, 64:96, :] for i, j in cells], 0)
        out.append(send(zs.at[k], gz.at[k], "gz", down[2]))
        cz[k - 1] = upper_z()
        out.append(send(cz.at[k - 1], uz.at[k - 1], "gz", up[2]))
        for i, j in cells:
            for a in range(3):
                if (i, j, a) not in done:
                    put(i, j, a)
        return out

    def ghosts(k, sign):
        for j in range(EY):
            hx[k, j] = keep(has_up[0], gx[k, j] + sign * cx[k - 1, j] if k > 0 else gx[k, j])
        for i in range(EX):
            hy[k, i] = keep(has_up[1], gy[k, i] + sign * cy[k - 1, i] if k > 0 else gy[k, i])
        hz[k] = keep(has_up[2], gz[k] + sign * cz[k - 1] if k > 0 else gz[k])

    def complete(p, out, k, sign):
        for n, (i, j) in enumerate(cells):
            along_x, along_y, along_z = p[i, j, 0:32, :], p[i, j, 32:64, :], p[i, j, 64:96, :]
            if i == 0:
                along_x = along_x + sign * keep(has_down[0], ux[k - 1, j])
            if j == 0:
                along_y = along_y + sign * keep(has_down[1], uy[k - 1, i])
            below = jnp.where(lane == 0, unpack(uz[k - 1], n, 0), 0.0)
            along_z = along_z + sign * keep(has_down[2], below)
            out[i, j, 0:32, :] = along_x
            out[i, j, 32:64, :] = along_y
            out[i, j, 64:96, :] = along_z

    for a in range(3):
        loads[a].wait()
        for n, (i, j) in enumerate(cells):
            X[i, j, 32 * a : 32 * a + 32, :] = xn[pl.ds(256 * a + n, FD, stride=CELLS), :]
    zs[0] = pack([X[i, j, 64:96, :] for i, j in cells], 0)
    pl.semaphore_wait(barrier, partners)
    copies = old_exchange(0, X)
    copies.append(send(zs.at[0], gz.at[0], "gz", down[2]))
    known_1 = announce(know.at[0], near)
    for copy in loads[3:9]:
        copy.wait()
    s = sf[...]
    high = s.astype(BF16)
    SH[...] = high
    SL[...] = (s - high.astype(F32)).astype(BF16)
    for n in range(0, 3072, 128):
        FN[n : n + 128, :] = fb[n : n + 128, :].astype(F32)
    for copy in copies:
        copy.wait_recv()
    pl.semaphore_wait(know.at[0], known_1)
    known_2 = announce(know.at[1], [(axis, step) for axis in range(2) for step in (2, -2)])
    ghosts(0, 0.0)

    def residual(i, j, a):
        n = i * EY + j
        load = bn[pl.ds(a * FD * CELLS + n, FD, stride=CELLS), :]
        return load - diag(a, n) * X[i, j, 32 * a : 32 * a + 32, :] - gathered(i, j, a)

    copies = round_trip(X, PR, 1, residual)

    def volume(n):
        pair = [FN[pl.ds(n + m, 384, stride=CELLS), :] for m in range(2)]
        moved = dot(vb[...], jnp.concatenate([p.astype(BF16) for p in pair], axis=1))
        for m in range(2):
            coarse = 1.0 - fi[n + m : n + m + 1, :].astype(F32)
            BASE[n + m] = pair[m] + TIME_STEP * (coarse * moved[:, EZ * m : EZ * m + EZ])

    loads[9].wait()
    volume(0)
    volume(2)
    for copy in copies:
        copy.wait_recv()
    if known_2:
        pl.semaphore_wait(know.at[1], known_2)
    known_3 = 1 + announce(know.at[2], [(2, 1), (2, -1), (2, 2)])
    pl.semaphore_signal(know.at[2], inc=1, device_id={"gx": other_core}, device_id_type=MESH)
    ghosts(1, -1.0)
    complete(PR, R0, 1, -1.0)

    def image(i, j, a):
        return diag(a, i * EY + j) * R0[i, j, 32 * a : 32 * a + 32, :] + gathered(i, j, a)

    copies = round_trip(R0, P0, 2, image)
    zero = jnp.zeros((8, EZ), F32)

    def over_ghosts(value):
        out = zero
        for j in range(EY):
            out = out + fold(value(hx[1, j], hx[2, j], cx[1, j], upper(j, 0)))
        for i in range(EX):
            out = out + fold(value(hy[1, i], hy[2, i], cy[1, i], upper(i, 1)))
        return out

    sum_a, sum_e00 = zero, zero
    for i, j in cells:
        r = R0[i, j]
        sum_a = sum_a + fold(r * r)
        sum_e00 = sum_e00 + fold(r * P0[i, j])
    sum_e00 = sum_e00 + over_ghosts(lambda r, w, c0, c1: r * c0) + fold(hz[1] * cz[1])
    a = total(sum_a)
    e00 = total(sum_e00)
    shift = jnp.where(a > 0.0, e00 / jnp.where(a > 0.0, a, 1.0), 0.0)
    volume(4)
    volume(6)
    loads[10].wait()
    LF[...] = ltb[...].astype(F32).T.astype(BF16)
    for copy in copies:
        copy.wait_recv()
    pl.semaphore_wait(know.at[2], known_3)
    ghosts(2, 1.0)
    complete(P0, W1, 2, 1.0)

    apply(W1, 2, 0)
    apply(W1, 2, 1)
    sum_b, sum_c, sum_e01, sum_e11 = zero, zero, zero, zero
    for n, (i, j) in enumerate(cells):
        for k in range(3):
            at = slice(32 * k, 32 * k + 32)
            r, w, p = R0[i, j, at, :], W1[i, j, at, :], P0[i, j, at, :]
            q = w - shift * r
            sum_b = sum_b + fold(r * q)
            sum_c = sum_c + fold(q * q)
            sum_e01 = sum_e01 + fold(q * p)
            sum_e11 = sum_e11 + fold(q * (diag(k, n) * w + gathered(i, j, k) - shift * p))
    top = upper_z()
    q = hz[2] - shift * hz[1]
    sum_e01 = sum_e01 + fold(q * cz[1]) + over_ghosts(lambda r, w, c0, c1: (w - shift * r) * c0)
    sum_e11 = sum_e11 + fold(q * (top - shift * cz[1]))
    sum_e11 = sum_e11 + over_ghosts(lambda r, w, c0, c1: (w - shift * r) * (c1 - shift * c0))
    row = lax.broadcasted_iota(jnp.int32, (8, EZ), 0)
    column = lax.broadcasted_iota(jnp.int32, (8, EZ), 1)
    tile = zero
    for n, value in [(2, sum_b), (3, sum_c), (5, sum_e01), (6, sum_e11)]:
        tile = jnp.where(row == n, jnp.sum(value, axis=0, keepdims=True), tile)
    tile = jnp.broadcast_to(jnp.sum(tile, axis=1, keepdims=True), (8, EZ))
    for n, value in [(0, shift), (1, a), (4, e00)]:
        tile = jnp.where(row == n, value, tile)
    planes, layers = sizes[0] // 2, max(sizes[1] // 2, 1)
    group = planes * sizes[2]
    place = lax.div(me[0], 2) + planes * me[2] + group * (core + 2 * lax.rem(me[1], layers))
    own[...] = jnp.where(column == place, tile, 0.0)

    def gather(k, source, landing, targets):
        for n, target in enumerate(targets):
            pltpu.make_async_remote_copy(
                src_ref=source, dst_ref=landing.at[n], send_sem=gather_send.at[k], recv_sem=gather_recv.at[k],
                device_id=target, device_id_type=MESH,
            ).start()
        out = source[...]
        pltpu.make_async_copy(landing, landing, gather_recv.at[k]).wait()
        for n in range(len(targets)):
            out = out + landing[n]
        return out

    tile = gather(0, own, ra, [
        {"gx": lax.rem(me[0] + 2 * y, sizes[0]), "gz": lax.rem(me[2] + z, sizes[2])} for y, z in across(sizes)
    ])
    low = me[1] < layers
    own_b[0:8, :] = keep(low, tile)
    own_b[8:16, :] = keep(jnp.logical_not(low), tile)
    tile = gather(1, own_b, rb, [
        {"gx": other_core if c else me[0], "gy": lax.rem(me[1] + z, sizes[1])} for c, z in along(sizes)
    ])

    moments[...] = tile
    for copy in started:
        copy.wait_send()
    pltpu.make_async_copy(ra, ra, gather_send.at[0]).wait()
    pltpu.make_async_copy(rb, rb, gather_send.at[1]).wait()


def finish(*refs):
    (moments, X, R0, W1, hx, hy, hz, BASE, LF, fi, fo_hbm, xo_hbm, GH, ON, FO, XO, new_v, new_x, new_y, new_z, out_sem) = refs
    cells = [(i, j) for i in range(EX) for j in range(EY)]
    lane = lax.broadcasted_iota(jnp.int32, (FD, EZ), 1)
    tile = moments[...]

    def summed(value):
        return jnp.sum(value(tile[0:8]) + value(tile[8:16]), axis=1, keepdims=True)

    norm0 = summed(lambda t: t[1:2])
    alpha0 = norm0 / summed(lambda t: t[4:5])

    def norm1_of(t):
        f = 1.0 - alpha0 * t[0:1]
        return f * f * t[1:2] - 2.0 * alpha0 * f * t[2:3] + alpha0 * alpha0 * t[3:4]

    norm1 = summed(norm1_of)
    beta = norm1 / norm0

    def energy_of(t):
        f = 1.0 + beta - alpha0 * t[0:1]
        return f * f * t[4:5] - 2.0 * alpha0 * f * t[5:6] + alpha0 * alpha0 * t[6:7]

    alpha1 = norm1 / summed(energy_of)
    on_r = alpha0 + alpha1 * (1.0 + beta)
    on_w = -alpha1 * alpha0

    for n, (i, j) in enumerate(cells):
        new = X[i, j] + on_r * R0[i, j] + on_w * W1[i, j]
        new_v[i, j] = new
        XO[pl.ds(n, 96, stride=CELLS), :] = new
    copies = [pltpu.make_async_copy(XO, xo_hbm, out_sem.at[0])]
    copies[0].start()
    for j in range(EY):
        new_x[j] = hx[0, j] + on_r * hx[1, j] + on_w * hx[2, j]
    for i in range(EX):
        new_y[i] = hy[0, i] + on_r * hy[1, i] + on_w * hy[2, i]
    new_z[...] = hz[0] + on_r * hz[1] + on_w * hz[2]
    for n, (i, j) in enumerate(cells):
        fine = fi[n : n + 1, :] > 0
        new_faces = faces_of(new_v, new_x, new_y, new_z, lane, i, j)
        old_faces = faces_of(X, hx.at[0], hy.at[0], hz.at[0], lane, i, j)
        for at, (new, old) in enumerate(zip(new_faces, old_faces)):
            GH[32 * at : 32 * at + 32, EZ * n : EZ * n + EZ] = jnp.where(fine, new, old).astype(BF16)
    rows = 384 // CHUNKS
    for chunk in range(CHUNKS):
        at = slice(rows * chunk, rows * chunk + rows)
        for n in range(0, CELLS, 2):
            lifted = dot(LF[at, :], GH[:, EZ * n : EZ * n + 2 * EZ])
            for m in range(2):
                ON[pl.ds(rows * CELLS * chunk + n + m, rows, stride=CELLS), :] = (
                    BASE[n + m, at, :] + TIME_STEP * lifted[:, EZ * m : EZ * m + EZ]
                )
        for n in range(rows * CELLS * chunk, rows * CELLS * (chunk + 1), 128):
            FO[n : n + 128, :] = ON[n : n + 128, :].astype(BF16)
        where = slice(rows * CELLS * chunk, rows * CELLS * (chunk + 1))
        copy = pltpu.make_async_copy(FO.at[where, :], fo_hbm.at[where, :], out_sem.at[1 + chunk])
        copy.start()
        copies.append(copy)
    for copy in copies:
        copy.wait()


def solution(mesh):
    sizes = tuple(mesh.shape[n] for n in ("gx", "gy", "gz"))

    def body(fields, trace_old, face_load, face_diag, fine_flag, coeff, volume_op, lift_op, schur_op):
        vmem = pltpu.VMEM
        field = (EX, EY, 96, EZ)
        copies = 3 + 6 + 6
        group, column = len(across(sizes)), len(along(sizes))
        scratch = [
            vmem((768, EZ), F32), vmem((768, EZ), F32), vmem((24, EZ), F32),
            vmem((8, EZ), F32), vmem((3072, EZ), BF16), vmem((384, 384), BF16), vmem((192, 384), BF16),
            vmem((192, 192), F32),
            vmem(field, F32), vmem(field, F32),
            vmem((CELLS, 192, EZ), F32), vmem((192, CELLS * EZ), BF16), vmem((192, CELLS * EZ), BF16),
            vmem((192, 192), BF16), vmem((192, 192), BF16),
            vmem((3072, EZ), F32),
            vmem((3, EY, FD, EZ), F32), vmem((3, EX, FD, EZ), F32), vmem((3, FD, EZ), F32),
            vmem((2, EY, FD, EZ), F32), vmem((2, EX, FD, EZ), F32), vmem((2, FD, EZ), F32),
            vmem((2, EY, FD, EZ), F32), vmem((2, EX, FD, EZ), F32), vmem((2, FD, EZ), F32),
            vmem((3, FD, EZ), F32),
            vmem((8, EZ), F32), vmem((group, 8, EZ), F32), vmem((16, EZ), F32), vmem((column, 16, EZ), F32),
            pltpu.SemaphoreType.DMA((11,)),
            pltpu.SemaphoreType.DMA((copies,)), pltpu.SemaphoreType.DMA((copies,)),
            pltpu.SemaphoreType.DMA((2,)), pltpu.SemaphoreType.DMA((2,)), pltpu.SemaphoreType.REGULAR((3,)),
        ]
        state = [
            ((16, EZ), F32), (field, F32), (field, F32), (field, F32),
            ((3, EY, FD, EZ), F32), ((3, EX, FD, EZ), F32), ((3, FD, EZ), F32),
            ((CELLS, 384, EZ), F32), ((384, 192), BF16), ((8, EZ), jnp.int32),
        ]
        in_vmem = pl.BlockSpec(memory_space=pltpu.VMEM)
        kept = pl.pallas_call(
            functools.partial(kernel, sizes),
            out_shape=[jax.ShapeDtypeStruct(*entry) for entry in state],
            in_specs=[pl.BlockSpec(memory_space=pltpu.HBM)] * 9,
            out_specs=[in_vmem] * len(state),
            scratch_shapes=scratch,
            compiler_params=pltpu.CompilerParams(
                collective_id=0, has_side_effects=True, vmem_limit_bytes=32 * 1024 * 1024
            ),
            name="step",
        )(
            *(
                pltpu.with_memory_space_constraint(value, pltpu.HBM)
                for value in (
                    trace_old.reshape(768, EZ), face_load.reshape(768, EZ), face_diag.reshape(24, EZ),
                    fine_flag.reshape(8, EZ), coeff.reshape(8, EZ), fields.reshape(3072, EZ), volume_op, lift_op.T,
                    schur_op,
                )
            )
        )
        out_f, out_x = pl.pallas_call(
            finish,
            out_shape=(jax.ShapeDtypeStruct((3072, EZ), BF16), jax.ShapeDtypeStruct((768, EZ), F32)),
            in_specs=[in_vmem] * len(state),
            out_specs=(pl.BlockSpec(memory_space=pltpu.HBM),) * 2,
            scratch_shapes=[
                vmem((192, CELLS * EZ), BF16), vmem((3072, EZ), F32), vmem((3072, EZ), BF16), vmem((768, EZ), F32),
                vmem(field, F32), vmem((EY, FD, EZ), F32), vmem((EX, FD, EZ), F32), vmem((FD, EZ), F32),
                pltpu.SemaphoreType.DMA((1 + CHUNKS,)),
            ],
            compiler_params=pltpu.CompilerParams(vmem_limit_bytes=24 * 1024 * 1024),
            name="finish",
        )(*kept)
        return out_f.reshape(fields.shape), out_x.reshape(trace_old.shape)

    return jax.shard_map(
        body,
        mesh=mesh,
        in_specs=(
            P(None, "gx", "gy", "gz"),
            P(None, None, "gx", "gy", "gz"),
            P(None, None, "gx", "gy", "gz"),
            P(None, "gx", "gy", "gz"),
            P("gx", "gy", "gz"),
            P("gx", "gy", "gz"),
            P(),
            P(),
            P(),
        ),
        out_specs=(P(None, "gx", "gy", "gz"), P(None, None, "gx", "gy", "gz")),
        check_vma=False,
    )
```

time: 35.4 us -> 34.9 us (0.986)
  local copies, waits for them, and re-layouts: 1.63 us -> 0 us
  Pallas kernels: 33.1 us -> 34.1 us
    unnamed x2 -> x0, local copies, waits for them, and re-layouts: 1.63 us -> none
    pallas_call x1 -> x2, Pallas kernels: 33.1 us -> 34.1 us  [the longest x1 32.3 us: body(): pl.pallas_call(functools.partial(kernel, sizes), out_shape=[jax.ShapeDtyp...]
where the time goes in v3:
time: 34.9 us; the launch traced here: 34.8 us
  Pallas kernels  34.1 us (98%)
  between operations  0.64 us (2%)
    pallas_call x1, Pallas kernels, body(): pl.pallas_call(functools.partial(kernel, sizes), out_shape=[jax.ShapeDtyp...  32.3 us
    pallas_call x1, Pallas kernels, body(): pl.pallas_call(finish, out_shape=(jax.ShapeDtypeStruct((3072, EZ), BF16),...  1.84 us

profile of v3, /device:TPU:1, one launch (start us, length us, event | category | flops | bytes accessed | tf_op | source)
XLA Modules:
  0.0 34.8 jit_solution(5642512550215521346)
XLA Ops:
  0.6 32.3 %step.1 = (f32[16,128]{1,0:T(8,128)S(1)}, f32[2,4,96,128]{3,2,1,0:T(8,128)S(1)}, f32[2,4,96,128]{3,2,1,0:T(8,128)S(1)}, f32[2,4,96,128]{3,2,1,0:T(8,128)S(1)}, f...) custom-call(f32[768,128]{1,0:T(8,128)} %bitcast.10, ...), custom_call_target="tpu_custom_call" | custom-call | tf_op jit(solution)/shard_map/step/pallas_call | solution.py:462
  32.9 1.8 %finish.1 = (bf16[3072,128]{1,0:T(8,128)(2,1)}, f32[768,128]{1,0:T(8,128)}) custom-call(f32[16,128]{1,0:T(8,128)S(1)} %get-tuple-element.14.refs_0_, f32[2,4,96,128]{3,2,1,0:T(8,128)S(1)} %get-tuple-element.15.refs_1_, f32[2,4,96,128]{3,2,1,0:T(8,128)S(1)} %get-tuple-element.16.refs_2_, f32[2,4,96,128]{3,2,1,0:T(8,128)S(1)} %get-tuple-element.17.refs_3_, ...), custom_call_target="tpu_custom_call" | custom-call | tf_op jit(solution)/shard_map/finish/pallas_call | solution.py:482

commit v4 on v3

--- a/solution.py
+++ b/solution.py
@@ -60,48 +60,56 @@
     (moments, X, R0, W1, hx, hy, hz, BASE, LF, fi) = refs[9:19]
     (xn, bn, dg, co, fb, vb, ltb, sf, PR, P0, T, GH, GL, SH, SL, FN,
      gx, gy, gz, ux, uy, uz, cx, cy, cz, zs, own, ra, own_b, rb,
+     wt, px, py, near_w, edge, pair_xy, corner, CH, CL,
      load_sem, send_sem, recv_sem, gather_send, gather_recv, know) = refs[19:]
     names = ("gx", "gy", "gz")
     me = [lax.axis_index(n) for n in names]
-    up = [lax.rem(m + 1, n) for m, n in zip(me, sizes)]
-    down = [lax.rem(m + n - 1, n) for m, n in zip(me, sizes)]
     has_up = [m < n - 1 for m, n in zip(me, sizes)]
     has_down = [m > 0 for m in me]
 
     barrier = pltpu.get_barrier_semaphore()
 
+    ring = [[m] + [lax.rem(m + k, n) for k in range(1, n)] for m, n in zip(me, sizes)]
+
+    def at(*steps):
+        return {
+            names[axis]: ring[axis][step % sizes[axis]] for axis, step in enumerate(steps) if step
+        }
+
     def announce(sem, steps):
         count = 0
-        for axis, step in steps:
-            n = sizes[axis]
-            if step % n:
-                target = lax.rem(me[axis] + step + n, n)
-                pl.semaphore_signal(sem, inc=1, device_id={names[axis]: target}, device_id_type=MESH)
+        for each in steps:
+            if any(step % n for step, n in zip(each, sizes)):
+                pl.semaphore_signal(sem, inc=1, device_id=at(*each), device_id_type=MESH)
                 count += 1
         return count
 
-    near = [(axis, step) for axis in range(3) for step in (1, -1)]
-    partners = announce(barrier, near)
+    near = [(1, 0, 0), (-1, 0, 0), (0, 1, 0), (0, -1, 0), (0, 0, 1), (0, 0, -1)]
+    both = [(p, q) for p in (1, -1) for q in (1, -1)]
+    diagonal = [(p, q, 0) for p, q in both] + [(p, 0, q) for p, q in both] + [(0, p, q) for p, q in both]
     loads = [
         pltpu.make_async_copy(src, dst, load_sem.at[k])
         for k, (src, dst) in enumerate(
             [(x_hbm.at[256 * a : 256 * a + 256, :], xn.at[256 * a : 256 * a + 256, :]) for a in range(3)]
-            + [(s_hbm, sf), (fine_hbm, fi), (coeff_hbm, co), (diag_hbm, dg), (b_hbm, bn),
+            + [(fine_hbm, fi), (coeff_hbm, co), (s_hbm, sf), (diag_hbm, dg), (b_hbm, bn),
                (f_hbm, fb), (v_hbm, vb), (lt_hbm, ltb)]
         )
     ]
-    for copy in loads:
+    for copy in loads[:3]:
+        copy.start()
+    partners = announce(barrier, near + diagonal)
+    for copy in loads[3:8]:
         copy.start()
     core = lax.rem(me[0], 2)
     other_core = me[0] + 1 - 2 * core
 
     started = []
 
-    def send(src, dst, name, target):
+    def send(src, dst, *steps):
         k = len(started)
         copy = pltpu.make_async_remote_copy(
             src_ref=src, dst_ref=dst, send_sem=send_sem.at[k], recv_sem=recv_sem.at[k],
-            device_id={name: target}, device_id_type=MESH,
+            device_id=at(*steps), device_id_type=MESH,
         )
         copy.start()
         started.append(copy)
@@ -113,10 +121,10 @@
     def keep(flag, value):
         return jnp.where(flag, value, 0.0)
 
-    def pack(pieces, at):
-        out = jnp.zeros((FD, EZ), F32)
-        for n, piece in enumerate(pieces):
-            out = jnp.where(lane == n, pltpu.roll(piece, (n - at) % EZ, 1), out)
+    def pack(pieces, lane_of, first=0, out=None):
+        out = jnp.zeros((FD, EZ), F32) if out is None else out
+        for n, piece in enumerate(pieces, first):
+            out = jnp.where(lane == n, pltpu.roll(piece, (n - lane_of) % EZ, 1), out)
         return out
 
     def faces(v, k, i, j):
@@ -139,7 +147,7 @@
                 T[n + m] = product[:, EZ * m : EZ * m + EZ] * weight(n + m)
 
     def weight(n):
-        return fi[n : n + 1, :].astype(F32) * co[n : n + 1, :]
+        return wt[n : n + 1, :]
 
     def gathered(i, j, a):
         n = i * EY + j
@@ -164,12 +172,6 @@
     def diag(a, n):
         return dg[a * CELLS + n : a * CELLS + n + 1, :]
 
-    def old_exchange(k, p):
-        return [
-            send(p.at[0, :, 0:32, :], gx.at[k], "gx", down[0]),
-            send(p.at[:, 0, 32:64, :], gy.at[k], "gy", down[1]),
-        ]
-
     def round_trip(v, p, k, partial):
         out = []
         done = set()
@@ -181,35 +183,35 @@
         apply(v, k - 1, 0)
         for j in range(EY):
             put(0, j, 0)
-        out.append(send(p.at[0, :, 0:32, :], gx.at[k], "gx", down[0]))
+        out.append(send(p.at[0, :, 0:32, :], gx.at[k], -1, 0, 0))
         apply(v, k - 1, 1)
         for j in range(EY):
             cx[k - 1, j] = upper(j, 0)
-        out.append(send(cx.at[k - 1], ux.at[k - 1], "gx", up[0]))
+        out.append(send(cx.at[k - 1], ux.at[k - 1], 1, 0, 0))
         for i in range(EX):
             put(i, 0, 1)
-        out.append(send(p.at[:, 0, 32:64, :], gy.at[k], "gy", down[1]))
+        out.append(send(p.at[:, 0, 32:64, :], gy.at[k], 0, -1, 0))
         for i in range(EX):
             cy[k - 1, i] = upper(i, 1)
-        out.append(send(cy.at[k - 1], uy.at[k - 1], "gy", up[1]))
+        out.append(send(cy.at[k - 1], uy.at[k - 1], 0, 1, 0))
         for i, j in cells:
             put(i, j, 2)
         zs[k] = pack([p[i, j, 64:96, :] for i, j in cells], 0)
-        out.append(send(zs.at[k], gz.at[k], "gz", down[2]))
+        out.append(send(zs.at[k], gz.at[k], 0, 0, -1))
         cz[k - 1] = upper_z()
-        out.append(send(cz.at[k - 1], uz.at[k - 1], "gz", up[2]))
+        out.append(send(cz.at[k - 1], uz.at[k - 1], 0, 0, 1))
         for i, j in cells:
             for a in range(3):
                 if (i, j, a) not in done:
                     put(i, j, a)
         return out
 
-    def ghosts(k, sign):
+    def ghosts(k, own_x, own_y, own_z):
         for j in range(EY):
-            hx[k, j] = keep(has_up[0], gx[k, j] + sign * cx[k - 1, j] if k > 0 else gx[k, j])
+            hx[k, j] = keep(has_up[0], gx[k, j] + own_x(j))
         for i in range(EX):
-            hy[k, i] = keep(has_up[1], gy[k, i] + sign * cy[k - 1, i] if k > 0 else gy[k, i])
-        hz[k] = keep(has_up[2], gz[k] + sign * cz[k - 1] if k > 0 else gz[k])
+            hy[k, i] = keep(has_up[1], gy[k, i] + own_y(i))
+        hz[k] = keep(has_up[2], gz[k] + own_z())
 
     def complete(p, out, k, sign):
         for n, (i, j) in enumerate(cells):
@@ -228,31 +230,78 @@
         loads[a].wait()
         for n, (i, j) in enumerate(cells):
             X[i, j, 32 * a : 32 * a + 32, :] = xn[pl.ds(256 * a + n, FD, stride=CELLS), :]
-    zs[0] = pack([X[i, j, 64:96, :] for i, j in cells], 0)
+    low_x = [X[0, j, 0:32, :] for j in range(EY)]
+    low_y = [X[i, 0, 32:64, :] for i in range(EX)]
+    low_z = [X[i, j, 64:96, :] for i, j in cells]
+    zs[0] = pack(low_y, 0, 12, pack(low_x, 0, 8, pack(low_z, 0)))
+    edge[...] = pack(low_y, EZ - 1, 12, pack(low_x, EZ - 1, 8))
     pl.semaphore_wait(barrier, partners)
-    copies = old_exchange(0, X)
-    copies.append(send(zs.at[0], gz.at[0], "gz", down[2]))
-    known_1 = announce(know.at[0], near)
-    for copy in loads[3:9]:
+    copies = [
+        send(X.at[0, 0, 0:64, :], pair_xy, -1, -1, 0),
+        send(X.at[1, 0, 32:64, :], corner.at[0], 1, -1, 0),
+        send(X.at[0, EY - 1, 0:32, :], corner.at[1], -1, 1, 0),
+        send(zs.at[0], corner.at[2], -1, 0, -1),
+        send(zs.at[0], corner.at[3], 1, 0, -1),
+        send(edge, corner.at[4], -1, 0, 1),
+        send(zs.at[0], corner.at[5], 0, -1, -1),
+        send(zs.at[0], corner.at[6], 0, 1, -1),
+        send(edge, corner.at[7], 0, -1, 1),
+        send(X.at[0, :, 0:32, :], gx.at[0], -1, 0, 0),
+        send(X.at[:, 0, 32:64, :], gy.at[0], 0, -1, 0),
+        send(zs.at[0], gz.at[0], 0, 0, -1),
+    ]
+    for copy in loads[8:]:
+        copy.start()
+    for copy in loads[3:8]:
         copy.wait()
+    wt[...] = fi[...].astype(F32) * co[...]
     s = sf[...]
     high = s.astype(BF16)
     SH[...] = high
     SL[...] = (s - high.astype(F32)).astype(BF16)
-    for n in range(0, 3072, 128):
-        FN[n : n + 128, :] = fb[n : n + 128, :].astype(F32)
-    for copy in copies:
-        copy.wait_recv()
-    pl.semaphore_wait(know.at[0], known_1)
-    known_2 = announce(know.at[1], [(axis, step) for axis in range(2) for step in (2, -2)])
-    ghosts(0, 0.0)
+    hx[0] = jnp.zeros((EY, FD, EZ), F32)
+    hy[0] = jnp.zeros((EX, FD, EZ), F32)
+    hz[0] = jnp.zeros((FD, EZ), F32)
 
     def residual(i, j, a):
         n = i * EY + j
         load = bn[pl.ds(a * FD * CELLS + n, FD, stride=CELLS), :]
         return load - diag(a, n) * X[i, j, 32 * a : 32 * a + 32, :] - gathered(i, j, a)
 
-    copies = round_trip(X, PR, 1, residual)
+    apply(X, 0, 0)
+    for j in range(EY):
+        px[j] = residual(0, j, 0)
+    copies.append(send(px, gx.at[1], -1, 0, 0))
+    apply(X, 0, 1)
+    for j in range(EY):
+        cx[0, j] = upper(j, 0)
+    copies.append(send(cx.at[0], ux.at[0], 1, 0, 0))
+    for i in range(EX):
+        py[i] = residual(i, 0, 1)
+        cy[0, i] = upper(i, 1)
+    copies.append(send(py, gy.at[1], 0, -1, 0))
+    copies.append(send(cy.at[0], uy.at[0], 0, 1, 0))
+    zs[1] = pack([residual(i, j, 2) for i, j in cells], 0)
+    cz[0] = upper_z()
+    copies.append(send(zs.at[1], gz.at[1], 0, 0, -1))
+    copies.append(send(cz.at[0], uz.at[0], 0, 0, 1))
+    for n, step in enumerate(near):
+        copies.append(send(wt, near_w.at[n], *step))
+    known_1 = announce(know.at[0], near)
+
+    def put(block, first, value):
+        cols = slice(first, first + value.shape[1])
+        high = value.astype(BF16)
+        CH[32 * block : 32 * block + 32, cols] = high
+        CL[32 * block : 32 * block + 32, cols] = (value - high.astype(F32)).astype(BF16)
+
+    CH[...] = jnp.zeros(CH.shape, BF16)
+    CL[...] = jnp.zeros(CL.shape, BF16)
+    for j in range(EY):
+        put(1, EZ * j, low_x[j])
+    for i in range(EX):
+        put(3, 1024 + EZ * i, low_y[i])
+    put(5, 1536, zs[0])
 
     def volume(n):
         pair = [FN[pl.ds(n + m, 384, stride=CELLS), :] for m in range(2)]
@@ -261,22 +310,94 @@
             coarse = 1.0 - fi[n + m : n + m + 1, :].astype(F32)
             BASE[n + m] = pair[m] + TIME_STEP * (coarse * moved[:, EZ * m : EZ * m + EZ])
 
+    loads[8].wait()
+    for n in range(0, 3072, 128):
+        FN[n : n + 128, :] = fb[n : n + 128, :].astype(F32)
     loads[9].wait()
     volume(0)
     volume(2)
-    for copy in copies:
+    for copy in copies[:12]:
         copy.wait_recv()
-    if known_2:
-        pl.semaphore_wait(know.at[1], known_2)
-    known_3 = 1 + announce(know.at[2], [(2, 1), (2, -1), (2, 2)])
-    pl.semaphore_signal(know.at[2], inc=1, device_id={"gx": other_core}, device_id_type=MESH)
-    ghosts(1, -1.0)
-    complete(PR, R0, 1, -1.0)
+    ghosts(0, lambda j: 0.0, lambda i: 0.0, lambda: 0.0)
+
+    def last(packed, n):
+        return jnp.where(lane == EZ - 1, unpack(packed, n, EZ - 1), 0.0)
+
+    def moved(packed, n, to):
+        return jnp.where(lane == to, unpack(packed, n, to), 0.0)
+
+    def over(axis, value):
+        return keep(has_up[axis], value)
+
+    put(3, 384, over(1, corner[0]))
+    put(3, 896, over(1, pair_xy[32:64, :]))
+    put(1, 1152, over(0, corner[1]))
+    put(1, 1408, over(0, pair_xy[0:32, :]))
+    for j in range(EY):
+        put(5, EZ * j, over(2, last(corner[3], EY + j)))
+        put(5, 512 + EZ * j, over(2, last(corner[2], j)))
+    for i in range(EX):
+        put(5, 1024 + EZ * i, over(2, last(corner[6], i * EY + EY - 1)))
+        put(5, 1280 + EZ * i, over(2, last(corner[5], i * EY)))
+    second = jnp.logical_and(lane >= EY, lane < 2 * EY)
+    put(1, 1536, over(0, jnp.where(second, pltpu.roll(corner[4], EZ - 4, 1), 0.0)))
+    put(1, 1664, over(0, jnp.where(second, pltpu.roll(corner[2], EZ - 4, 1), 0.0)))
+    put(3, 1536, over(1, moved(corner[7], 12, EY - 1) + moved(corner[7], 13, 2 * EY - 1)))
+    put(3, 1664, over(1, moved(corner[5], 12, EY - 1) + moved(corner[5], 13, 2 * EY - 1)))
+
+    def correction(block, first, size):
+        rows, cols = slice(32 * block, 32 * block + 32), slice(first, first + size)
+        high = CH[:, cols]
+        return dot(SH[rows, :], high) + (dot(SH[rows, :], CL[:, cols]) + dot(SL[rows, :], high))
+
+    def ends(n, at):
+        out = jnp.zeros((1, EZ), F32)
+        for c in range(CELLS):
+            out = jnp.where(lane[0:1] == c, jnp.broadcast_to(near_w[n, c : c + 1, at : at + 1], (1, EZ)), out)
+        return out
+
+    def cut(value, n):
+        return value[:, EZ * n : EZ * n + EZ]
+
+    xl, xh = correction(1, 0, 512), correction(0, 512, 512)
+    yl, yh = correction(3, 1024, 256), correction(2, 1280, 256)
+    zl, zh = correction(5, 1536, 128), correction(4, 1664, 128)
+    apply(X, 0, 0)
+    apply(X, 0, 1)
+    for i, j in cells:
+        for a in range(3):
+            PR[i, j, 32 * a : 32 * a + 32, :] = residual(i, j, a)
+    for copy in copies[12:]:
+        copy.wait_recv()
+    pl.semaphore_wait(know.at[0], known_1)
+
+    xl = [cut(xl, j) * near_w[0, EY + j : EY + j + 1, :] for j in range(EY)]
+    xh = [cut(xh, j) * near_w[1, j : j + 1, :] for j in range(EY)]
+    yl = [cut(yl, i) * near_w[2, i * EY + EY - 1 : i * EY + EY, :] for i in range(EX)]
+    yh = [cut(yh, i) * near_w[3, i * EY : i * EY + 1, :] for i in range(EX)]
+    zl = zl * ends(4, EZ - 1)
+    zh = zh * ends(5, 0)
+
+    for n, (i, j) in enumerate(cells):
+        along_x, along_y, along_z = PR[i, j, 0:32, :], PR[i, j, 32:64, :], PR[i, j, 64:96, :]
+        if i == 0:
+            along_x = along_x - keep(has_down[0], ux[0, j] + xl[j])
+        if j == 0:
+            along_y = along_y - keep(has_down[1], uy[0, i] + yl[i])
+        below = jnp.where(lane == 0, unpack(uz[0] + zl, n, 0), 0.0)
+        R0[i, j, 0:32, :] = along_x
+        R0[i, j, 32:64, :] = along_y
+        R0[i, j, 64:96, :] = along_z - keep(has_down[2], below)
+    ghosts(1, lambda j: -xh[j] - upper(j, 0), lambda i: -yh[i] - upper(i, 1), lambda: -zh - upper_z())
 
     def image(i, j, a):
         return diag(a, i * EY + j) * R0[i, j, 32 * a : 32 * a + 32, :] + gathered(i, j, a)
 
+    early = list(started)
     copies = round_trip(R0, P0, 2, image)
+    known_2 = announce(know.at[1], [(2, 0, 0), (-2, 0, 0), (0, 2, 0), (0, -2, 0), (2, 0, 1), (-2, 0, -1)])
+    for copy in early:
+        copy.wait_send()
     zero = jnp.zeros((8, EZ), F32)
 
     def over_ghosts(value):
@@ -302,8 +423,9 @@
     LF[...] = ltb[...].astype(F32).T.astype(BF16)
     for copy in copies:
         copy.wait_recv()
-    pl.semaphore_wait(know.at[2], known_3)
-    ghosts(2, 1.0)
+    if known_2:
+        pl.semaphore_wait(know.at[1], known_2)
+    ghosts(2, lambda j: cx[1, j], lambda i: cy[1, i], lambda: cz[1])
     complete(P0, W1, 2, 1.0)
 
     apply(W1, 2, 0)
@@ -324,44 +446,41 @@
     sum_e11 = sum_e11 + fold(q * (top - shift * cz[1]))
     sum_e11 = sum_e11 + over_ghosts(lambda r, w, c0, c1: (w - shift * r) * (c1 - shift * c0))
     row = lax.broadcasted_iota(jnp.int32, (8, EZ), 0)
-    column = lax.broadcasted_iota(jnp.int32, (8, EZ), 1)
+    column = lax.broadcasted_iota(jnp.int32, (1, EZ), 1)
     tile = zero
     for n, value in [(2, sum_b), (3, sum_c), (5, sum_e01), (6, sum_e11)]:
         tile = jnp.where(row == n, jnp.sum(value, axis=0, keepdims=True), tile)
     tile = jnp.broadcast_to(jnp.sum(tile, axis=1, keepdims=True), (8, EZ))
     for n, value in [(0, shift), (1, a), (4, e00)]:
         tile = jnp.where(row == n, value, tile)
-    planes, layers = sizes[0] // 2, max(sizes[1] // 2, 1)
-    group = planes * sizes[2]
-    place = lax.div(me[0], 2) + planes * me[2] + group * (core + 2 * lax.rem(me[1], layers))
-    own[...] = jnp.where(column == place, tile, 0.0)
-
-    def gather(k, source, landing, targets):
+    place = lax.div(me[0], 2) + sizes[0] // 2 * me[2]
+    mine = lax.broadcasted_iota(jnp.int32, (8, EZ), 1) == 16 * row + place
+    own[...] = jnp.sum(jnp.where(mine, tile, 0.0), axis=0, keepdims=True)
+
+    def gather(k, source, landing, targets, sent):
         for n, target in enumerate(targets):
             pltpu.make_async_remote_copy(
                 src_ref=source, dst_ref=landing.at[n], send_sem=gather_send.at[k], recv_sem=gather_recv.at[k],
                 device_id=target, device_id_type=MESH,
             ).start()
-        out = source[...]
+        sent()
         pltpu.make_async_copy(landing, landing, gather_recv.at[k]).wait()
-        for n in range(len(targets)):
-            out = out + landing[n]
-        return out
-
-    tile = gather(0, own, ra, [
-        {"gx": lax.rem(me[0] + 2 * y, sizes[0]), "gz": lax.rem(me[2] + z, sizes[2])} for y, z in across(sizes)
-    ])
-    low = me[1] < layers
-    own_b[0:8, :] = keep(low, tile)
-    own_b[8:16, :] = keep(jnp.logical_not(low), tile)
-    tile = gather(1, own_b, rb, [
-        {"gx": other_core if c else me[0], "gy": lax.rem(me[1] + z, sizes[1])} for c, z in along(sizes)
-    ])
-
+
+    gather(0, own, ra, [
+        {"gx": ring[0][2 * y], "gz": ring[2][z]} for y, z in across(sizes)
+    ], lambda: [copy.wait_send() for copy in copies])
+    total_row = own[...]
+    for n in range(ra.shape[0]):
+        total_row = total_row + ra[n]
+    own_b[...] = total_row
+    gather(1, own_b, rb, [
+        {"gx": other_core if c else me[0], "gy": ring[1][z]} for c, z in along(sizes)
+    ], lambda: pltpu.make_async_copy(ra, ra, gather_send.at[0]).wait())
+    rows = lax.broadcasted_iota(jnp.int32, (16, EZ), 0)
+    tile = jnp.where(rows == 0, total_row, 0.0)
+    for n in range(rb.shape[0]):
+        tile = jnp.where(rows == n + 1, rb[n], tile)
     moments[...] = tile
-    for copy in started:
-        copy.wait_send()
-    pltpu.make_async_copy(ra, ra, gather_send.at[0]).wait()
     pltpu.make_async_copy(rb, rb, gather_send.at[1]).wait()
 
 
@@ -371,24 +490,24 @@
     lane = lax.broadcasted_iota(jnp.int32, (FD, EZ), 1)
     tile = moments[...]
 
+    held = lax.broadcasted_iota(jnp.int32, (16, EZ), 1) < 16
+
+    def number(n):
+        return jnp.where(held, pltpu.roll(tile, EZ - 16 * n, 1) if n else tile, 0.0)
+
+    shift, a, b, c, e00, e01, e11 = [number(n) for n in range(7)]
+
     def summed(value):
-        return jnp.sum(value(tile[0:8]) + value(tile[8:16]), axis=1, keepdims=True)
-
-    norm0 = summed(lambda t: t[1:2])
-    alpha0 = norm0 / summed(lambda t: t[4:5])
-
-    def norm1_of(t):
-        f = 1.0 - alpha0 * t[0:1]
-        return f * f * t[1:2] - 2.0 * alpha0 * f * t[2:3] + alpha0 * alpha0 * t[3:4]
-
-    norm1 = summed(norm1_of)
+        return jnp.sum(jnp.sum(value, axis=0, keepdims=True), axis=1, keepdims=True)
+
+    norm0, energy0 = summed(a), summed(e00)
+    alpha0 = norm0 / energy0
+    f = 1.0 - alpha0 * shift
+    norm1 = summed(f * f * a - 2.0 * alpha0 * f * b + alpha0 * alpha0 * c)
+    energy1 = summed(f * f * e00 - 2.0 * alpha0 * f * e01 + alpha0 * alpha0 * e11)
+    mixed = summed(f * e00 - alpha0 * e01)
     beta = norm1 / norm0
-
-    def energy_of(t):
-        f = 1.0 + beta - alpha0 * t[0:1]
-        return f * f * t[4:5] - 2.0 * alpha0 * f * t[5:6] + alpha0 * alpha0 * t[6:7]
-
-    alpha1 = norm1 / summed(energy_of)
+    alpha1 = norm1 / (energy1 + 2.0 * beta * mixed + beta * beta * energy0)
     on_r = alpha0 + alpha1 * (1.0 + beta)
     on_w = -alpha1 * alpha0
 
@@ -434,7 +553,7 @@
     def body(fields, trace_old, face_load, face_diag, fine_flag, coeff, volume_op, lift_op, schur_op):
         vmem = pltpu.VMEM
         field = (EX, EY, 96, EZ)
-        copies = 3 + 6 + 6
+        copies = 12 + 6 + 6 + 6
         group, column = len(across(sizes)), len(along(sizes))
         scratch = [
             vmem((768, EZ), F32), vmem((768, EZ), F32), vmem((24, EZ), F32),
@@ -448,10 +567,12 @@
             vmem((2, EY, FD, EZ), F32), vmem((2, EX, FD, EZ), F32), vmem((2, FD, EZ), F32),
             vmem((2, EY, FD, EZ), F32), vmem((2, EX, FD, EZ), F32), vmem((2, FD, EZ), F32),
             vmem((3, FD, EZ), F32),
-            vmem((8, EZ), F32), vmem((group, 8, EZ), F32), vmem((16, EZ), F32), vmem((column, 16, EZ), F32),
+            vmem((1, EZ), F32), vmem((group, 1, EZ), F32), vmem((1, EZ), F32), vmem((column, 1, EZ), F32),
+            vmem((8, EZ), F32), vmem((EY, FD, EZ), F32), vmem((EX, FD, EZ), F32), vmem((6, 8, EZ), F32), vmem((FD, EZ), F32), vmem((64, EZ), F32), vmem((8, FD, EZ), F32),
+            vmem((192, 1792), BF16), vmem((192, 1792), BF16),
             pltpu.SemaphoreType.DMA((11,)),
             pltpu.SemaphoreType.DMA((copies,)), pltpu.SemaphoreType.DMA((copies,)),
-            pltpu.SemaphoreType.DMA((2,)), pltpu.SemaphoreType.DMA((2,)), pltpu.SemaphoreType.REGULAR((3,)),
+            pltpu.SemaphoreType.DMA((2,)), pltpu.SemaphoreType.DMA((2,)), pltpu.SemaphoreType.REGULAR((2,)),
         ]
         state = [
             ((16, EZ), F32), (field, F32), (field, F32), (field, F32),

time: 34.9 us -> 34 us (0.974)
  Pallas kernels: 34.1 us -> 33.2 us
    pallas_call x1, Pallas kernels: 32.3 us -> 31.5 us  [body(): pl.pallas_call(functools.partial(kernel, sizes), out_shape=[jax.ShapeDtyp...]
where the time goes in v4:
time: 34 us; the launch traced here: 33.8 us
  Pallas kernels  33.2 us (98%)
  between operations  0.64 us (2%)
    pallas_call x1, Pallas kernels, body(): pl.pallas_call(functools.partial(kernel, sizes), out_shape=[jax.ShapeDtyp...  31.5 us
    pallas_call x1, Pallas kernels, body(): pl.pallas_call(finish, out_shape=(jax.ShapeDtypeStruct((3072, EZ), BF16),...  1.72 us

profile of v4, /device:TPU:1, one launch (start us, length us, event | category | flops | bytes accessed | tf_op | source)
XLA Modules:
  0.0 33.8 jit_solution(9770939964688857408)
XLA Ops:
  0.6 31.5 %step.1 = (f32[16,128]{1,0:T(8,128)S(1)}, f32[2,4,96,128]{3,2,1,0:T(8,128)S(1)}, f32[2,4,96,128]{3,2,1,0:T(8,128)S(1)}, f32[2,4,96,128]{3,2,1,0:T(8,128)S(1)}, f...) custom-call(f32[768,128]{1,0:T(8,128)} %bitcast.10, ...), custom_call_target="tpu_custom_call" | custom-call | tf_op jit(solution)/shard_map/step/pallas_call | solution.py:583
  32.1 1.7 %finish.1 = (bf16[3072,128]{1,0:T(8,128)(2,1)}, f32[768,128]{1,0:T(8,128)}) custom-call(f32[16,128]{1,0:T(8,128)S(1)} %get-tuple-element.14.refs_0_, f32[2,4,96,128]{3,2,1,0:T(8,128)S(1)} %get-tuple-element.15.refs_1_, f32[2,4,96,128]{3,2,1,0:T(8,128)S(1)} %get-tuple-element.16.refs_2_, f32[2,4,96,128]{3,2,1,0:T(8,128)S(1)} %get-tuple-element.17.refs_3_, ...), custom_call_target="tpu_custom_call" | custom-call | tf_op jit(solution)/shard_map/finish/pallas_call | solution.py:603

commit v5 on v4

--- a/solution.py
+++ b/solution.py
@@ -40,6 +40,18 @@
 
 def unpack(packed, n, at):
     return pltpu.roll(packed, (at - n) % EZ, 1)
+
+
+def squeeze(value):
+    out = value[0:8, :]
+    for n in range(1, 4):
+        out = out + pltpu.roll(value[8 * n : 8 * n + 8, :], 16 * n, 1)
+    return out
+
+
+def spread(value):
+    wide = jnp.concatenate([value] + [pltpu.roll(value, EZ - 16 * n, 1) for n in range(1, 4)], axis=0)
+    return jnp.where(lax.broadcasted_iota(jnp.int32, wide.shape, 1) < 16, wide, 0.0)
 
 
 def faces_of(v, hx, hy, hz, lane, i, j):
@@ -58,9 +70,9 @@
 def kernel(sizes, *refs):
     (x_hbm, b_hbm, diag_hbm, fine_hbm, coeff_hbm, f_hbm, v_hbm, lt_hbm, s_hbm) = refs[:9]
     (moments, X, R0, W1, hx, hy, hz, BASE, LF, fi) = refs[9:19]
-    (xn, bn, dg, co, fb, vb, ltb, sf, PR, P0, T, GH, GL, SH, SL, FN,
-     gx, gy, gz, ux, uy, uz, cx, cy, cz, zs, own, ra, own_b, rb,
-     wt, px, py, near_w, edge, pair_xy, corner, CH, CL,
+    (xn, bn, dg, co, fb, vb, ltb, sf, PR, P0, T, GH, GL, SX, FN,
+     gx, gy, gz, ux, uy, uz, cx, cy, cz, cs, zs, own, ra, own_b, rb,
+     wt, px, py, near_w, edge, pair_xy, corner, packed, CH, CL,
      load_sem, send_sem, recv_sem, gather_send, gather_recv, know) = refs[19:]
     names = ("gx", "gy", "gz")
     me = [lax.axis_index(n) for n in names]
@@ -130,21 +142,29 @@
     def faces(v, k, i, j):
         return faces_of(v, hx.at[k], hy.at[k], hz.at[k], lane, i, j)
 
-    def apply(v, k, half):
+    def convert(v, k, half, upper_only=False):
         for n, (i, j) in enumerate(cells):
             if i != half:
                 continue
+            fresh = (1,) * (i == EX - 1) + (3,) * (j == EY - 1) + (5,) if upper_only else range(6)
             for at, block in enumerate(faces(v, k, i, j)):
+                if at not in fresh:
+                    continue
                 high = block.astype(BF16)
                 low = (block - high.astype(F32)).astype(BF16)
                 GH[32 * at : 32 * at + 32, EZ * n : EZ * n + EZ] = high
                 GL[32 * at : 32 * at + 32, EZ * n : EZ * n + EZ] = low
+    def multiply(half):
         for n in range(EY * half, EY * half + EY, 2):
             cols = slice(EZ * n, EZ * n + 2 * EZ)
-            high = GH[:, cols]
-            product = dot(SH[...], high) + (dot(SH[...], GL[:, cols]) + dot(SL[...], high))
+            both = dot(SX[...], GH[:, cols])
+            product = both[0:192, :] + (dot(SX[0:192, :], GL[:, cols]) + both[192:384, :])
             for m in range(2):
                 T[n + m] = product[:, EZ * m : EZ * m + EZ] * weight(n + m)
+
+    def apply(v, k, half):
+        convert(v, k, half)
+        multiply(half)
 
     def weight(n):
         return wt[n : n + 1, :]
@@ -196,10 +216,11 @@
         out.append(send(cy.at[k - 1], uy.at[k - 1], 0, 1, 0))
         for i, j in cells:
             put(i, j, 2)
-        zs[k] = pack([p[i, j, 64:96, :] for i, j in cells], 0)
+        zs[k] = squeeze(pack([p[i, j, 64:96, :] for i, j in cells], 0))
         out.append(send(zs.at[k], gz.at[k], 0, 0, -1))
-        cz[k - 1] = upper_z()
-        out.append(send(cz.at[k - 1], uz.at[k - 1], 0, 0, 1))
+        cz[...] = upper_z()
+        cs[k - 1] = squeeze(cz[...])
+        out.append(send(cs.at[k - 1], uz.at[k - 1], 0, 0, 1))
         for i, j in cells:
             for a in range(3):
                 if (i, j, a) not in done:
@@ -211,16 +232,17 @@
             hx[k, j] = keep(has_up[0], gx[k, j] + own_x(j))
         for i in range(EX):
             hy[k, i] = keep(has_up[1], gy[k, i] + own_y(i))
-        hz[k] = keep(has_up[2], gz[k] + own_z())
+        hz[k] = keep(has_up[2], spread(gz[k]) + own_z())
 
     def complete(p, out, k, sign):
+        from_z = spread(uz[k - 1])
         for n, (i, j) in enumerate(cells):
             along_x, along_y, along_z = p[i, j, 0:32, :], p[i, j, 32:64, :], p[i, j, 64:96, :]
             if i == 0:
                 along_x = along_x + sign * keep(has_down[0], ux[k - 1, j])
             if j == 0:
                 along_y = along_y + sign * keep(has_down[1], uy[k - 1, i])
-            below = jnp.where(lane == 0, unpack(uz[k - 1], n, 0), 0.0)
+            below = jnp.where(lane == 0, unpack(from_z, n, 0), 0.0)
             along_z = along_z + sign * keep(has_down[2], below)
             out[i, j, 0:32, :] = along_x
             out[i, j, 32:64, :] = along_y
@@ -233,20 +255,21 @@
     low_x = [X[0, j, 0:32, :] for j in range(EY)]
     low_y = [X[i, 0, 32:64, :] for i in range(EX)]
     low_z = [X[i, j, 64:96, :] for i, j in cells]
-    zs[0] = pack(low_y, 0, 12, pack(low_x, 0, 8, pack(low_z, 0)))
-    edge[...] = pack(low_y, EZ - 1, 12, pack(low_x, EZ - 1, 8))
+    low = pack(low_y, 0, 12, pack(low_x, 0, 8, pack(low_z, 0)))
+    zs[0] = squeeze(low)
+    edge[...] = squeeze(pack(low_y, EZ - 1, 12, pack(low_x, EZ - 1, 8)))
     pl.semaphore_wait(barrier, partners)
     copies = [
+        send(X.at[0, :, 0:32, :], gx.at[0], -1, 0, 0),
         send(X.at[0, 0, 0:64, :], pair_xy, -1, -1, 0),
         send(X.at[1, 0, 32:64, :], corner.at[0], 1, -1, 0),
         send(X.at[0, EY - 1, 0:32, :], corner.at[1], -1, 1, 0),
-        send(zs.at[0], corner.at[2], -1, 0, -1),
-        send(zs.at[0], corner.at[3], 1, 0, -1),
-        send(edge, corner.at[4], -1, 0, 1),
-        send(zs.at[0], corner.at[5], 0, -1, -1),
-        send(zs.at[0], corner.at[6], 0, 1, -1),
-        send(edge, corner.at[7], 0, -1, 1),
-        send(X.at[0, :, 0:32, :], gx.at[0], -1, 0, 0),
+        send(zs.at[0], packed.at[0], -1, 0, -1),
+        send(zs.at[0], packed.at[1], 1, 0, -1),
+        send(edge, packed.at[2], -1, 0, 1),
+        send(zs.at[0], packed.at[3], 0, -1, -1),
+        send(zs.at[0], packed.at[4], 0, 1, -1),
+        send(edge, packed.at[5], 0, -1, 1),
         send(X.at[:, 0, 32:64, :], gy.at[0], 0, -1, 0),
         send(zs.at[0], gz.at[0], 0, 0, -1),
     ]
@@ -257,8 +280,8 @@
     wt[...] = fi[...].astype(F32) * co[...]
     s = sf[...]
     high = s.astype(BF16)
-    SH[...] = high
-    SL[...] = (s - high.astype(F32)).astype(BF16)
+    SX[0:192, :] = high
+    SX[192:384, :] = (s - high.astype(F32)).astype(BF16)
     hx[0] = jnp.zeros((EY, FD, EZ), F32)
     hy[0] = jnp.zeros((EX, FD, EZ), F32)
     hz[0] = jnp.zeros((FD, EZ), F32)
@@ -281,10 +304,10 @@
         cy[0, i] = upper(i, 1)
     copies.append(send(py, gy.at[1], 0, -1, 0))
     copies.append(send(cy.at[0], uy.at[0], 0, 1, 0))
-    zs[1] = pack([residual(i, j, 2) for i, j in cells], 0)
-    cz[0] = upper_z()
+    zs[1] = squeeze(pack([residual(i, j, 2) for i, j in cells], 0))
+    cs[0] = squeeze(upper_z())
     copies.append(send(zs.at[1], gz.at[1], 0, 0, -1))
-    copies.append(send(cz.at[0], uz.at[0], 0, 0, 1))
+    copies.append(send(cs.at[0], uz.at[0], 0, 0, 1))
     for n, step in enumerate(near):
         copies.append(send(wt, near_w.at[n], *step))
     known_1 = announce(know.at[0], near)
@@ -301,7 +324,7 @@
         put(1, EZ * j, low_x[j])
     for i in range(EX):
         put(3, 1024 + EZ * i, low_y[i])
-    put(5, 1536, zs[0])
+    put(5, 1536, low)
 
     def volume(n):
         pair = [FN[pl.ds(n + m, 384, stride=CELLS), :] for m in range(2)]
@@ -329,26 +352,29 @@
     def over(axis, value):
         return keep(has_up[axis], value)
 
+    apart = [spread(packed[n]) for n in range(6)]
     put(3, 384, over(1, corner[0]))
     put(3, 896, over(1, pair_xy[32:64, :]))
     put(1, 1152, over(0, corner[1]))
     put(1, 1408, over(0, pair_xy[0:32, :]))
     for j in range(EY):
-        put(5, EZ * j, over(2, last(corner[3], EY + j)))
-        put(5, 512 + EZ * j, over(2, last(corner[2], j)))
+        put(5, EZ * j, over(2, last(apart[1], EY + j)))
+        put(5, 512 + EZ * j, over(2, last(apart[0], j)))
     for i in range(EX):
-        put(5, 1024 + EZ * i, over(2, last(corner[6], i * EY + EY - 1)))
-        put(5, 1280 + EZ * i, over(2, last(corner[5], i * EY)))
+        put(5, 1024 + EZ * i, over(2, last(apart[4], i * EY + EY - 1)))
+        put(5, 1280 + EZ * i, over(2, last(apart[3], i * EY)))
     second = jnp.logical_and(lane >= EY, lane < 2 * EY)
-    put(1, 1536, over(0, jnp.where(second, pltpu.roll(corner[4], EZ - 4, 1), 0.0)))
-    put(1, 1664, over(0, jnp.where(second, pltpu.roll(corner[2], EZ - 4, 1), 0.0)))
-    put(3, 1536, over(1, moved(corner[7], 12, EY - 1) + moved(corner[7], 13, 2 * EY - 1)))
-    put(3, 1664, over(1, moved(corner[5], 12, EY - 1) + moved(corner[5], 13, 2 * EY - 1)))
-
-    def correction(block, first, size):
-        rows, cols = slice(32 * block, 32 * block + 32), slice(first, first + size)
-        high = CH[:, cols]
-        return dot(SH[rows, :], high) + (dot(SH[rows, :], CL[:, cols]) + dot(SL[rows, :], high))
+    put(1, 1536, over(0, jnp.where(second, pltpu.roll(apart[2], EZ - 4, 1), 0.0)))
+    put(1, 1664, over(0, jnp.where(second, pltpu.roll(apart[0], EZ - 4, 1), 0.0)))
+    put(3, 1536, over(1, moved(apart[5], 12, EY - 1) + moved(apart[5], 13, 2 * EY - 1)))
+    put(3, 1664, over(1, moved(apart[3], 12, EY - 1) + moved(apart[3], 13, 2 * EY - 1)))
+
+    def correction(pair, first, size):
+        rows, lower = slice(64 * pair, 64 * pair + 64), slice(192 + 64 * pair, 256 + 64 * pair)
+        cols = slice(first, first + 2 * size)
+        both = dot(jnp.concatenate([SX[rows, :], SX[lower, :]], axis=0), CH[:, cols])
+        out = both[0:64, :] + (dot(SX[rows, :], CL[:, cols]) + both[64:128, :])
+        return out[32:64, 0:size], out[0:32, size : 2 * size]
 
     def ends(n, at):
         out = jnp.zeros((1, EZ), F32)
@@ -359,11 +385,13 @@
     def cut(value, n):
         return value[:, EZ * n : EZ * n + EZ]
 
-    xl, xh = correction(1, 0, 512), correction(0, 512, 512)
-    yl, yh = correction(3, 1024, 256), correction(2, 1280, 256)
-    zl, zh = correction(5, 1536, 128), correction(4, 1664, 128)
-    apply(X, 0, 0)
-    apply(X, 0, 1)
+    xl, xh = correction(0, 0, 512)
+    yl, yh = correction(1, 1024, 256)
+    zl, zh = correction(2, 1536, 128)
+    convert(X, 0, 0, True)
+    convert(X, 0, 1, True)
+    multiply(0)
+    multiply(1)
     for i, j in cells:
         for a in range(3):
             PR[i, j, 32 * a : 32 * a + 32, :] = residual(i, j, a)
@@ -378,13 +406,14 @@
     zl = zl * ends(4, EZ - 1)
     zh = zh * ends(5, 0)
 
+    from_z = spread(uz[0]) + zl
     for n, (i, j) in enumerate(cells):
         along_x, along_y, along_z = PR[i, j, 0:32, :], PR[i, j, 32:64, :], PR[i, j, 64:96, :]
         if i == 0:
             along_x = along_x - keep(has_down[0], ux[0, j] + xl[j])
         if j == 0:
             along_y = along_y - keep(has_down[1], uy[0, i] + yl[i])
-        below = jnp.where(lane == 0, unpack(uz[0] + zl, n, 0), 0.0)
+        below = jnp.where(lane == 0, unpack(from_z, n, 0), 0.0)
         R0[i, j, 0:32, :] = along_x
         R0[i, j, 32:64, :] = along_y
         R0[i, j, 64:96, :] = along_z - keep(has_down[2], below)
@@ -413,7 +442,7 @@
         r = R0[i, j]
         sum_a = sum_a + fold(r * r)
         sum_e00 = sum_e00 + fold(r * P0[i, j])
-    sum_e00 = sum_e00 + over_ghosts(lambda r, w, c0, c1: r * c0) + fold(hz[1] * cz[1])
+    sum_e00 = sum_e00 + over_ghosts(lambda r, w, c0, c1: r * c0) + fold(hz[1] * cz[...])
     a = total(sum_a)
     e00 = total(sum_e00)
     shift = jnp.where(a > 0.0, e00 / jnp.where(a > 0.0, a, 1.0), 0.0)
@@ -425,7 +454,7 @@
         copy.wait_recv()
     if known_2:
         pl.semaphore_wait(know.at[1], known_2)
-    ghosts(2, lambda j: cx[1, j], lambda i: cy[1, i], lambda: cz[1])
+    ghosts(2, lambda j: cx[1, j], lambda i: cy[1, i], lambda: cz[...])
     complete(P0, W1, 2, 1.0)
 
     apply(W1, 2, 0)
@@ -442,8 +471,8 @@
             sum_e11 = sum_e11 + fold(q * (diag(k, n) * w + gathered(i, j, k) - shift * p))
     top = upper_z()
     q = hz[2] - shift * hz[1]
-    sum_e01 = sum_e01 + fold(q * cz[1]) + over_ghosts(lambda r, w, c0, c1: (w - shift * r) * c0)
-    sum_e11 = sum_e11 + fold(q * (top - shift * cz[1]))
+    sum_e01 = sum_e01 + fold(q * cz[...]) + over_ghosts(lambda r, w, c0, c1: (w - shift * r) * c0)
+    sum_e11 = sum_e11 + fold(q * (top - shift * cz[...]))
     sum_e11 = sum_e11 + over_ghosts(lambda r, w, c0, c1: (w - shift * r) * (c1 - shift * c0))
     row = lax.broadcasted_iota(jnp.int32, (8, EZ), 0)
     column = lax.broadcasted_iota(jnp.int32, (1, EZ), 1)
@@ -561,14 +590,15 @@
             vmem((192, 192), F32),
             vmem(field, F32), vmem(field, F32),
             vmem((CELLS, 192, EZ), F32), vmem((192, CELLS * EZ), BF16), vmem((192, CELLS * EZ), BF16),
-            vmem((192, 192), BF16), vmem((192, 192), BF16),
+            vmem((384, 192), BF16),
             vmem((3072, EZ), F32),
-            vmem((3, EY, FD, EZ), F32), vmem((3, EX, FD, EZ), F32), vmem((3, FD, EZ), F32),
-            vmem((2, EY, FD, EZ), F32), vmem((2, EX, FD, EZ), F32), vmem((2, FD, EZ), F32),
-            vmem((2, EY, FD, EZ), F32), vmem((2, EX, FD, EZ), F32), vmem((2, FD, EZ), F32),
-            vmem((3, FD, EZ), F32),
+            vmem((3, EY, FD, EZ), F32), vmem((3, EX, FD, EZ), F32), vmem((3, 8, EZ), F32),
+            vmem((2, EY, FD, EZ), F32), vmem((2, EX, FD, EZ), F32), vmem((2, 8, EZ), F32),
+            vmem((2, EY, FD, EZ), F32), vmem((2, EX, FD, EZ), F32), vmem((FD, EZ), F32), vmem((2, 8, EZ), F32),
+            vmem((3, 8, EZ), F32),
             vmem((1, EZ), F32), vmem((group, 1, EZ), F32), vmem((1, EZ), F32), vmem((column, 1, EZ), F32),
-            vmem((8, EZ), F32), vmem((EY, FD, EZ), F32), vmem((EX, FD, EZ), F32), vmem((6, 8, EZ), F32), vmem((FD, EZ), F32), vmem((64, EZ), F32), vmem((8, FD, EZ), F32),
+            vmem((8, EZ), F32), vmem((EY, FD, EZ), F32), vmem((EX, FD, EZ), F32), vmem((6, 8, EZ), F32), vmem((8, EZ), F32), vmem((64, EZ), F32), vmem((2, FD, EZ), F32),
+            vmem((6, 8, EZ), F32),
             vmem((192, 1792), BF16), vmem((192, 1792), BF16),
             pltpu.SemaphoreType.DMA((11,)),
             pltpu.SemaphoreType.DMA((copies,)), pltpu.SemaphoreType.DMA((copies,)),

time: 34 us -> 33.7 us (level)
  no operation moved by 1% of the time
where the time goes in v5:
time: 33.7 us; the launch traced here: 33.6 us
  Pallas kernels  33 us (98%)
  between operations  0.64 us (2%)
    pallas_call x1, Pallas kernels, body(): pl.pallas_call(functools.partial(kernel, sizes), out_shape=[jax.ShapeDtyp...  31.3 us
    pallas_call x1, Pallas kernels, body(): pl.pallas_call(finish, out_shape=(jax.ShapeDtypeStruct((3072, EZ), BF16),...  1.72 us

profile of v5, /device:TPU:1, one launch (start us, length us, event | category | flops | bytes accessed | tf_op | source)
XLA Modules:
  0.0 33.6 jit_solution(14763043875165272387)
XLA Ops:
  0.6 31.3 %step.1 = (f32[16,128]{1,0:T(8,128)S(1)}, f32[2,4,96,128]{3,2,1,0:T(8,128)S(1)}, f32[2,4,96,128]{3,2,1,0:T(8,128)S(1)}, f32[2,4,96,128]{3,2,1,0:T(8,128)S(1)}, f...) custom-call(f32[768,128]{1,0:T(8,128)} %bitcast.10, ...), custom_call_target="tpu_custom_call" | custom-call | tf_op jit(solution)/shard_map/step/pallas_call | solution.py:613
  31.9 1.7 %finish.1 = (bf16[3072,128]{1,0:T(8,128)(2,1)}, f32[768,128]{1,0:T(8,128)}) custom-call(f32[16,128]{1,0:T(8,128)S(1)} %get-tuple-element.14.refs_0_, f32[2,4,96,128]{3,2,1,0:T(8,128)S(1)} %get-tuple-element.15.refs_1_, f32[2,4,96,128]{3,2,1,0:T(8,128)S(1)} %get-tuple-element.16.refs_2_, f32[2,4,96,128]{3,2,1,0:T(8,128)S(1)} %get-tuple-element.17.refs_3_, ...), custom_call_target="tpu_custom_call" | custom-call | tf_op jit(solution)/shard_map/finish/pallas_call | solution.py:633

commit v6 on v5

--- a/solution.py
+++ b/solution.py
@@ -482,7 +482,7 @@
     tile = jnp.broadcast_to(jnp.sum(tile, axis=1, keepdims=True), (8, EZ))
     for n, value in [(0, shift), (1, a), (4, e00)]:
         tile = jnp.where(row == n, value, tile)
-    place = lax.div(me[0], 2) + sizes[0] // 2 * me[2]
+    place = core + 2 * me[1]
     mine = lax.broadcasted_iota(jnp.int32, (8, EZ), 1) == 16 * row + place
     own[...] = jnp.sum(jnp.where(mine, tile, 0.0), axis=0, keepdims=True)
 
@@ -496,14 +496,14 @@
         pltpu.make_async_copy(landing, landing, gather_recv.at[k]).wait()
 
     gather(0, own, ra, [
-        {"gx": ring[0][2 * y], "gz": ring[2][z]} for y, z in across(sizes)
+        {"gx": other_core if c else me[0], "gy": ring[1][z]} for c, z in along(sizes)
     ], lambda: [copy.wait_send() for copy in copies])
     total_row = own[...]
     for n in range(ra.shape[0]):
         total_row = total_row + ra[n]
     own_b[...] = total_row
     gather(1, own_b, rb, [
-        {"gx": other_core if c else me[0], "gy": ring[1][z]} for c, z in along(sizes)
+        {"gx": ring[0][2 * y], "gz": ring[2][z]} for y, z in across(sizes)
     ], lambda: pltpu.make_async_copy(ra, ra, gather_send.at[0]).wait())
     rows = lax.broadcasted_iota(jnp.int32, (16, EZ), 0)
     tile = jnp.where(rows == 0, total_row, 0.0)
@@ -596,7 +596,7 @@
             vmem((2, EY, FD, EZ), F32), vmem((2, EX, FD, EZ), F32), vmem((2, 8, EZ), F32),
             vmem((2, EY, FD, EZ), F32), vmem((2, EX, FD, EZ), F32), vmem((FD, EZ), F32), vmem((2, 8, EZ), F32),
             vmem((3, 8, EZ), F32),
-            vmem((1, EZ), F32), vmem((group, 1, EZ), F32), vmem((1, EZ), F32), vmem((column, 1, EZ), F32),
+            vmem((1, EZ), F32), vmem((column, 1, EZ), F32), vmem((1, EZ), F32), vmem((group, 1, EZ), F32),
             vmem((8, EZ), F32), vmem((EY, FD, EZ), F32), vmem((EX, FD, EZ), F32), vmem((6, 8, EZ), F32), vmem((8, EZ), F32), vmem((64, EZ), F32), vmem((2, FD, EZ), F32),
             vmem((6, 8, EZ), F32),
             vmem((192, 1792), BF16), vmem((192, 1792), BF16),

time: 33.7 us -> 32.9 us (0.976)
  Pallas kernels: 33 us -> 32.1 us
    pallas_call x1, Pallas kernels: 31.3 us -> 30.4 us  [body(): pl.pallas_call(functools.partial(kernel, sizes), out_shape=[jax.ShapeDtyp...]
where the time goes in v6:
time: 32.9 us; the launch traced here: 32.8 us
  Pallas kernels  32.1 us (98%)
  between operations  0.64 us (2%)
    pallas_call x1, Pallas kernels, body(): pl.pallas_call(functools.partial(kernel, sizes), out_shape=[jax.ShapeDtyp...  30.4 us
    pallas_call x1, Pallas kernels, body(): pl.pallas_call(finish, out_shape=(jax.ShapeDtypeStruct((3072, EZ), BF16),...  1.72 us

profile of v6, /device:TPU:1, one launch (start us, length us, event | category | flops | bytes accessed | tf_op | source)
XLA Modules:
  0.0 32.8 jit_solution(11004116446907417165)
XLA Ops:
  0.6 30.4 %step.1 = (f32[16,128]{1,0:T(8,128)S(1)}, f32[2,4,96,128]{3,2,1,0:T(8,128)S(1)}, f32[2,4,96,128]{3,2,1,0:T(8,128)S(1)}, f32[2,4,96,128]{3,2,1,0:T(8,128)S(1)}, f...) custom-call(f32[768,128]{1,0:T(8,128)} %bitcast.10, ...), custom_call_target="tpu_custom_call" | custom-call | tf_op jit(solution)/shard_map/step/pallas_call | solution.py:613
  31.0 1.7 %finish.1 = (bf16[3072,128]{1,0:T(8,128)(2,1)}, f32[768,128]{1,0:T(8,128)}) custom-call(f32[16,128]{1,0:T(8,128)S(1)} %get-tuple-element.14.refs_0_, f32[2,4,96,128]{3,2,1,0:T(8,128)S(1)} %get-tuple-element.15.refs_1_, f32[2,4,96,128]{3,2,1,0:T(8,128)S(1)} %get-tuple-element.16.refs_2_, f32[2,4,96,128]{3,2,1,0:T(8,128)S(1)} %get-tuple-element.17.refs_3_, ...), custom_call_target="tpu_custom_call" | custom-call | tf_op jit(solution)/shard_map/finish/pallas_call | solution.py:633

commit v7 on v6

--- a/solution.py
+++ b/solution.py
@@ -333,12 +333,6 @@
             coarse = 1.0 - fi[n + m : n + m + 1, :].astype(F32)
             BASE[n + m] = pair[m] + TIME_STEP * (coarse * moved[:, EZ * m : EZ * m + EZ])
 
-    loads[8].wait()
-    for n in range(0, 3072, 128):
-        FN[n : n + 128, :] = fb[n : n + 128, :].astype(F32)
-    loads[9].wait()
-    volume(0)
-    volume(2)
     for copy in copies[:12]:
         copy.wait_recv()
     ghosts(0, lambda j: 0.0, lambda i: 0.0, lambda: 0.0)
@@ -446,10 +440,6 @@
     a = total(sum_a)
     e00 = total(sum_e00)
     shift = jnp.where(a > 0.0, e00 / jnp.where(a > 0.0, a, 1.0), 0.0)
-    volume(4)
-    volume(6)
-    loads[10].wait()
-    LF[...] = ltb[...].astype(F32).T.astype(BF16)
     for copy in copies:
         copy.wait_recv()
     if known_2:
@@ -495,9 +485,23 @@
         sent()
         pltpu.make_async_copy(landing, landing, gather_recv.at[k]).wait()
 
+    def under_gather():
+        for copy in copies:
+            copy.wait_send()
+        loads[8].wait()
+        for n in range(0, 3072, 128):
+            FN[n : n + 128, :] = fb[n : n + 128, :].astype(F32)
+        loads[9].wait()
+        volume(0)
+        volume(2)
+        volume(4)
+        volume(6)
+        loads[10].wait()
+        LF[...] = ltb[...].astype(F32).T.astype(BF16)
+
     gather(0, own, ra, [
         {"gx": other_core if c else me[0], "gy": ring[1][z]} for c, z in along(sizes)
-    ], lambda: [copy.wait_send() for copy in copies])
+    ], under_gather)
     total_row = own[...]
     for n in range(ra.shape[0]):
         total_row = total_row + ra[n]

time: 32.9 us -> 32.9 us (level)
  no operation moved by 1% of the time
where the time goes in v7:
time: 32.9 us; the launch traced here: 32.8 us
  Pallas kernels  32.1 us (98%)
  between operations  0.64 us (2%)
    pallas_call x1, Pallas kernels, body(): pl.pallas_call(functools.partial(kernel, sizes), out_shape=[jax.ShapeDtyp...  30.4 us
    pallas_call x1, Pallas kernels, body(): pl.pallas_call(finish, out_shape=(jax.ShapeDtypeStruct((3072, EZ), BF16),...  1.72 us

profile of v7, /device:TPU:1, one launch (start us, length us, event | category | flops | bytes accessed | tf_op | source)
XLA Modules:
  0.0 32.8 jit_solution(15011657735009969536)
XLA Ops:
  0.6 30.4 %step.1 = (f32[16,128]{1,0:T(8,128)S(1)}, f32[2,4,96,128]{3,2,1,0:T(8,128)S(1)}, f32[2,4,96,128]{3,2,1,0:T(8,128)S(1)}, f32[2,4,96,128]{3,2,1,0:T(8,128)S(1)}, f...) custom-call(f32[768,128]{1,0:T(8,128)} %bitcast.10, ...), custom_call_target="tpu_custom_call" | custom-call | tf_op jit(solution)/shard_map/step/pallas_call | solution.py:617
  31.0 1.7 %finish.1 = (bf16[3072,128]{1,0:T(8,128)(2,1)}, f32[768,128]{1,0:T(8,128)}) custom-call(f32[16,128]{1,0:T(8,128)S(1)} %get-tuple-element.14.refs_0_, f32[2,4,96,128]{3,2,1,0:T(8,128)S(1)} %get-tuple-element.15.refs_1_, f32[2,4,96,128]{3,2,1,0:T(8,128)S(1)} %get-tuple-element.16.refs_2_, f32[2,4,96,128]{3,2,1,0:T(8,128)S(1)} %get-tuple-element.17.refs_3_, ...), custom_call_target="tpu_custom_call" | custom-call | tf_op jit(solution)/shard_map/finish/pallas_call | solution.py:637
